TPU v7x, 32 devices: a whole 2x2x4 slice. The times are simulated.
32 devices in a mesh: member: 4 (over x, core), space: 8 (over z, y).
Axes of the slice: x: 2, y: 2, z: 4, core: 2. Of those that a mesh axis runs over, the one named last changes fastest.
Arguments:
- features: bfloat16 [4, 641, 192, 128], P('member', None, 'space'), may hold values from -6 to 6
- depth_kernel: float32 [641, 5, 5], replicated, may hold values from -1.25 to 1.25
- in_weight: bfloat16 [641, 1282], replicated, may hold values from -0.25 to 0.25
- out_weight: bfloat16 [1282, 641], replicated, may hold values from -0.15625 to 0.15625
- decoder_weight: bfloat16 [641, 72], replicated, may hold values from -0.25 to 0.25
- observed: float32 [72, 192, 128], P(None, 'space'), may hold values from -6 to 6
- land_mask: int32 [192, 128], P('space'), may hold values 0 or 1
Outputs:
- grad_features: bfloat16 [4, 641, 192, 128], P('member', None, 'space')
- decoder_grad: float32 [641, 72], replicated
All inputs are finite; a program needn't handle non-finite values. No bound on the sum of `land_mask` on one device may be relied on, other than what follows from the above.
Results may differ from a plain program's by a relative error of at most 0.0054.
Values may be sent and summed in bfloat16 or wider, within the bound.
A program may use at most 128 MiB of HBM per device.

v0:
```python
import math

import jax
import jax.numpy as jnp
from jax import lax
from jax.sharding import PartitionSpec as P

norm_eps = 1e-05


def padded_2(cells, sides, width):
    for axis, dim in sides:
        count = lax.axis_size(axis)
        head = lax.slice_in_dim(cells, 0, width, axis=dim)
        tail = lax.slice_in_dim(cells, cells.shape[dim] - width, cells.shape[dim], axis=dim)
        cells = jnp.concatenate(
            [
                lax.ppermute(tail, axis, [(i, (i + 1) % count) for i in range(count)]),
                cells,
                lax.ppermute(head, axis, [((i + 1) % count, i) for i in range(count)]),
            ],
            axis=dim,
        )
    return cells


def per_device(features, depth_kernel, in_weight, out_weight, decoder_weight, observed, land_mask):
    channels = features.shape[1]
    lon_len = features.shape[2]
    lat_len = features.shape[3]
    points = lon_len * lat_len
    padded = padded_2(features, (("space", 2),), 2)
    widened = jnp.pad(padded.astype(jnp.float32), ((0, 0), (0, 0), (0, 0), (2, 2)))
    convolved = jnp.zeros(features.shape, jnp.float32)
    for row_off in range(5):
        for col_off in range(5):
            convolved = (
                convolved
                + depth_kernel[:, row_off, col_off][None, :, None, None]
                * widened[:, :, row_off : row_off + lon_len, col_off : col_off + lat_len]
            )
    center = jnp.mean(convolved, axis=1, keepdims=True)
    shifted = convolved - center
    normed = (
        shifted * lax.rsqrt(jnp.mean(shifted * shifted, axis=1, keepdims=True) + norm_eps)
    ).astype(jnp.bfloat16)
    flat = normed.reshape(channels, points)
    hidden = jax.nn.gelu(
        jnp.einsum("ch,cp->hp", in_weight, flat, preferred_element_type=jnp.float32),
        approximate=False,
    ).astype(jnp.bfloat16)
    mlp_out = jnp.einsum("hc,hp->cp", out_weight, hidden, preferred_element_type=jnp.float32)
    block_out = (features.reshape(channels, points).astype(jnp.float32) + mlp_out).astype(
        jnp.bfloat16
    )
    decoded_flat = jnp.einsum(
        "co,cp->op", decoder_weight, block_out, preferred_element_type=jnp.float32
    ).astype(jnp.bfloat16)
    outputs = decoded_flat.shape[0]
    decoded = decoded_flat.reshape(1, outputs, lon_len, lat_len)
    groups = lax.axis_size("member")
    members = features.shape[0] * groups
    point_weight = 4.0 + 8.0 * land_mask.astype(jnp.float32)
    own_f = decoded.astype(jnp.float32)
    apart = own_f - lax.all_gather(decoded, "member", axis=0, tiled=True).astype(jnp.float32)
    apart_norm = jnp.sqrt(jnp.sum(apart * apart, axis=1, keepdims=True) + 1.0)
    pair_sum = jnp.sum(apart / apart_norm, axis=0, keepdims=True)
    misfit = own_f - observed[None]
    misfit_norm = jnp.sqrt(jnp.sum(misfit * misfit, axis=1, keepdims=True) + 1.0)
    score_grad = (point_weight[None, None] * (misfit / misfit_norm - pair_sum / members)).astype(
        jnp.bfloat16
    )
    grad_flat = score_grad.reshape(outputs, points)
    grad_features = jnp.einsum(
        "co,op->cp", decoder_weight, grad_flat, preferred_element_type=jnp.float32
    ).astype(jnp.bfloat16)
    total_points = lon_len * lax.axis_size("space") * lat_len
    term = jnp.einsum(
        "cp,op->co", block_out, grad_flat, preferred_element_type=jnp.float32
    ) / math.sqrt(members * total_points)
    decoder_grad = lax.psum(term, ("member", "space"))
    return (grad_features.reshape(features.shape), decoder_grad)


def solution(mesh):
    placed = (
        P("member", None, "space", None),
        P(),
        P(),
        P(),
        P(),
        P(None, "space", None),
        P("space", None),
    )
    return jax.shard_map(
        per_device,
        mesh=mesh,
        in_specs=placed,
        out_specs=(P("member", None, "space", None), P()),
        check_vma=False,
    )
```

profile of v0, /device:TPU:0, one launch (start us, length us, event | category | flops | bytes accessed | tf_op | source)
XLA Modules:
  0.0 392.8 jit_solution(12034791294327075821)
XLA Ops:
  7.2 0.0 copy-start
  7.2 0.0 all-gather.2.cloned.1.call-start
  7.2 2.3 fusion.106
  9.6 3.0 collective-permute-start
  12.7 3.1 collective-permute-start.1
  15.8 2.6 convert_bitcast_fusion
  18.5 0.5 pad.8
  19.0 0.0 copy-start.8
  19.0 0.0 copy-start.5
  19.0 5.0 %copy.15 = f32[81,8,24,128]{3,1,2,0:T(8,128)} copy(f32[81,8,24,128]{3,2,1,0:T(8,128)S(1)} %bitcast.131) | data formatting | bytes 15925248
  24.0 0.1 slice_reduce_fusion.23
  24.1 0.2 slice_reduce_fusion.24
  24.2 2.6 collective-permute-done
  26.8 0.3 copy.11
  27.1 2.0 collective-permute-done.1
  29.1 0.3 copy.12
  29.4 6.9 %maximum_convert_fusion = f32[1,641,28,128]{3,2,1,0:T(8,128)} fusion(bf16[1,641,2,128]{3,2,1,0:T(2,128)(2,1)S(1)} %copy.12, bf16[1,641,24,128]{3,2,1,0:T(8,128)(2,1)S(1)} %copy-done.5, bf16[1,641,2,128]{3,2,1,0:T(2,128)(2,1)S(1)} %copy.11), kind=kLoop, calls=%fused_computation.100 | loop fusion | flops 13784064 | bytes 13784064 | tf_op jit(solution)/shard_map/convert_element_type | solution.py:33
  36.3 130.6 %fusion.104 = (f32[24,128]{1,0:T(8,128)S(1)}, f32[1,641,24,128]{3,2,1,0:T(8,128)}) fusion(f32[641]{0:T(1024)S(1)} %get-tuple-element.25, f32[641]{0:T(1024)S(1)} %get-tuple-element.26, f32[1,641,28,128]{3,2,1,0:T(8,128)} %maximum_convert_fusion, f32[641]{0:T(1024)S(1)} %get-tuple-element.3, f32[641]{0:T(1024)S(1)} %get-tuple-element.4, ...), kind=kLoop, calls=%fused_computation.177 | loop fusion | flops 98454528 | bytes 57838180 | tf_op jit(solution)/shard_map/reduce_sum | solution.py:42
  166.9 4.3 %multiply_reduce_fusion = f32[24,128]{1,0:T(8,128)S(1)} fusion(f32[1,641,24,128]{3,2,1,0:T(8,128)} %get-tuple-element.28, f32[24,128]{1,0:T(8,128)S(1)} %broadcast_multiply_fusion), kind=kLoop, calls=%fused_computation.99 | loop fusion | flops 5904384 | bytes 7901184 | tf_op jit(solution)/shard_map/reduce_sum | solution.py:45
  171.2 1.1 copy-done.2
  172.3 0.9 fusion.69
  173.2 0.7 pad.9
  173.9 1.1 copy.16
  175.1 0.0 slice-start.1
  175.1 0.0 copy-start.10
  175.1 42.9 %fusion.123 = bf16[1282,3072]{1,0:T(8,128)(2,1)S(1)} fusion(bf16[641,3072]{1,0:T(8,128)(2,1)S(1)} %bitcast.142, bf16[641,1282]{1,0:T(8,128)(2,1)S(1)} %copy-done), kind=kOutput, calls=%fused_computation.23.clone.clone.clone.clone.1 | convolution fusion | flops 5304895488 | bytes 13458436 | tf_op jit(solution)/shard_map/ch,cp->hp/dot_general | solution.py:49
  218.1 0.0 copy-start.7
  218.1 7.2 %fusion.18 = bf16[641,3072]{1,0:T(8,128)(2,1)S(1)} fusion(f32[641,3072]{1,0:T(8,128)S(1)} %bitcast.138, bf16[1282,641]{0,1:T(8,128)(2,1)S(1)} %copy-done.10, bf16[1282,3072]{1,0:T(8,128)(2,1)S(1)} %fusion.123), kind=kOutput, calls=%fused_computation.45 | convolution fusion | flops 5052844032 | bytes 21335044 | tf_op jit(solution)/shard_map/hc,hp->cp/dot_general | solution.py:52
  225.3 1.9 copy-done.3
  227.2 0.8 convolution_convert_fusion.1
  228.0 0.8 copy.18
  228.8 0.0 all-gather.2.cloned.1.call-update
  228.9 0.0 all-reduce.3.cloned.1.call-start
  228.9 0.1 convert_bitcast_fusion.1
  229.0 0.2 copy.17
  229.2 0.2 multiply_reduce_fusion.2
  229.3 20.6 %all-gather.2.cloned.1.call-done = bf16[4,72,24,128]{3,2,1,0:T(8,128)(2,1)} async-done(((bf16[1,72,24,128]{3,2,1,0:T(8,128)(2,1)}), bf16[4,72,24,128]{3,2,1,0:T(8,128)(2,1)}) %all-gather.2.cloned.1.call-update) | async-done | bytes 1769488 | tf_op jit(solution)/shard_map/all_gather | solution.py:65
  249.9 2.1 multiply_reduce_fusion.1
  252.0 2.0 divide_reduce_fusion
  254.1 0.2 multiply_convert_fusion.1
  254.3 2.0 convolution_multiply_fusion
  256.3 3.1 convolution_convert_fusion
  259.4 0.0 all-reduce.3.cloned.1.call-update
  259.5 0.0 copy-start.1
  259.5 3.4 copy.20
  262.9 2.6 slice_bitcast_fusion
  265.5 118.8 %all-reduce.3.cloned.1.call-done = f32[641,72]{0,1:T(8,128)} async-done(((f32[641,72]{0,1:T(8,128)}), f32[641,72]{0,1:T(8,128)}) %all-reduce.3.cloned.1.call-update) | async-done | bytes 184624 | tf_op jit(solution)/shard_map/psum | solution.py:81
  384.3 1.6 copy.30
  (24 shorter events, 0.2 us)
Async XLA Ops:
  7.2 167.9 %copy-start = (bf16[641,1282]{1,0:T(8,128)(2,1)S(1)}, bf16[641,1282]{1,0:T(8,128)(2,1)}, u32[]{:S(2)}) copy-start(bf16[641,1282]{1,0:T(8,128)(2,1)} %param.9) | copy-start | bytes 4930576
  7.2 242.7 %all-gather.2.cloned.1.call-start = ((), (), s32[]{:S(2)}) async-start(), calls=%async_computation | async-start | bytes 2211840 | tf_op jit(solution)/shard_map/all_gather | solution.py:65
  9.6 17.2 %collective-permute-start = (bf16[1,641,2,128]{3,1,2,0:T(8,128)(2,1)S(1)}, bf16[1,641,2,128]{3,1,2,0:T(8,128)(2,1)S(1)}, u32[]{:S(2)}, u32[]{:S(2)}) collective-permute-start(bf16[1,641,2,128]{3,1,2,0:T(8,128)(2,1)S(1)} %copy.13), channel_id=1, source_target_pairs={{0,1},{1,2},{2,3},{3,4},{4,5},{5,6},{6,7},{7,0},{8,9},{9,10},{10,1... | collective-permute-start | bytes 984584 | tf_op jit(solution)/shard_map/ppermute | solution.py:18
  12.7 16.4 %collective-permute-start.1 = (bf16[1,641,2,128]{3,1,2,0:T(8,128)(2,1)S(1)}, bf16[1,641,2,128]{3,1,2,0:T(8,128)(2,1)S(1)}, u32[]{:S(2)}, u32[]{:S(2)}) collective-permute-start(bf16[1,641,2,128]{3,1,2,0:T(8,128)(2,1)S(1)} %copy.14), channel_id=1, source_target_pairs={{1,0},{2,1},{3,2},{4,3},{5,4},{6,5},{7,6},{0,7},{9,8},{10,9},{11,1... | collective-permute-start | bytes 984584 | tf_op jit(solution)/shard_map/ppermute | solution.py:20
  19.0 5.0 %copy-start.8 = (f32[641,5,5]{0,2,1:T(8,128)S(1)}, f32[641,5,5]{0,2,1:T(8,128)}, u32[]{:S(2)}) copy-start(f32[641,5,5]{0,2,1:T(8,128)} %param.8) | copy-start | bytes 192304
  19.0 10.4 %copy-start.5 = (bf16[1,641,24,128]{3,2,1,0:T(8,128)(2,1)S(1)}, bf16[1,641,24,128]{3,2,1,0:T(8,128)(2,1)}, u32[]{:S(2)}) copy-start(bf16[1,641,24,128]{3,2,1,0:T(8,128)(2,1)} %param.7) | copy-start | bytes 11814916
  166.9 5.5 %copy-start.2 = (f32[1,641,24,128]{3,2,1,0:T(8,128)S(1)}, f32[1,641,24,128]{3,2,1,0:T(8,128)}, u32[]{:S(2)}) copy-start(f32[1,641,24,128]{3,2,1,0:T(8,128)} %get-tuple-element.28) | copy-start | bytes 23629828
  173.9 44.1 %slice-start = ((s8[7962624]{0:T(1024)(128)(4,1)}), s8[4194304]{0:T(1024)(128)(4,1)S(1)}, s32[]{:S(2)}) async-start(s8[7962624]{0:T(1024)(128)(4,1)} %bitcast.136), calls=%async_computation.2 | async-start | bytes 8388608
  175.1 43.0 %slice-start.1 = ((s8[7962624]{0:T(1024)(128)(4,1)}), s8[3768320]{0:T(1024)(128)(4,1)S(1)}, s32[]{:S(2)}) async-start(s8[7962624]{0:T(1024)(128)(4,1)} %bitcast.136), calls=%async_computation.3 | async-start | bytes 7536640
  175.1 43.0 %copy-start.10 = (bf16[1282,641]{0,1:T(8,128)(2,1)S(1)}, bf16[1282,641]{0,1:T(8,128)(2,1)}, u32[]{:S(2)}) copy-start(bf16[1282,641]{0,1:T(8,128)(2,1)} %param.10) | copy-start | bytes 4930576
  218.1 9.1 %copy-start.7 = (bf16[641,72]{0,1:T(8,128)(2,1)S(1)}, bf16[641,72]{0,1:T(8,128)(2,1)}, u32[]{:S(2)}) copy-start(bf16[641,72]{0,1:T(8,128)(2,1)} %param.11) | copy-start | bytes 276916
  225.3 1.9 copy-start.3
  227.2 1.9 copy-start.6
  227.2 2.1 copy-start.9
  228.9 155.4 %all-reduce.3.cloned.1.call-start = ((), (), s32[]{:S(2)}) async-start(), calls=%async_computation.1 | async-start | bytes 442368 | tf_op jit(solution)/shard_map/psum | solution.py:81
  249.9 4.4 %copy-start.4 = (bf16[641,3072]{1,0:T(8,128)(2,1)S(1)}, bf16[641,3072]{1,0:T(8,128)(2,1)}, u32[]{:S(2)}) copy-start(bf16[641,3072]{1,0:T(8,128)(2,1)} %copy-done.3) | copy-start | bytes 11814916
  259.5 126.5 %copy-start.1 = (bf16[641,1282]{1,0:T(8,128)(2,1)S(1)}, bf16[641,1282]{1,0:T(8,128)(2,1)}, u32[]{:S(2)}) copy-start(bf16[641,1282]{1,0:T(8,128)(2,1)} %param.9) | copy-start | bytes 4930576
Sparse Core Ops, SparseCore 0:
  229.0 20.8 all-gather.1
  259.6 124.6 all-reduce.2
where the time goes:
time: 393 us
  other arithmetic  150 us (38%)
  waiting for transfers between devices  144 us (37%)
  matrix products  56.1 us (14%)
  local copies, waits for them, and re-layouts  22.2 us (6%)
  between operations  14.3 us (4%)
  starting transfers between devices  6.24 us (2%)
    reduce_sum x1, other arithmetic, per_device(): center = jnp.mean(convolved, axis=1, keepdims=True)  131 us
    psum x1, waiting for transfers between devices, per_device(): decoder_grad = lax.psum(term, ('member', 'space'))  119 us
    dot_general x1, matrix products, per_device(): jnp.einsum('ch,cp->hp', in_weight, flat, preferred_element_type=jnp.float32)  42.9 us
    all_gather x1, waiting for transfers between devices, per_device(): lax.all_gather(decoded, 'member', axis=0, tiled=True).astype(jnp.float32)  20.6 us
    unnamed x36, local copies, waits for them, and re-layouts  16.6 us
  transfers between devices with their start and end apart: 4, of which 4 were waited for; matrix products, arithmetic and copies ran while one was open for 4% of the time, Pallas kernels for 0%

commit v1 on v0

v1 whole, which is shorter than its diff:
```python
import functools
import math

import jax
import jax.numpy as jnp
from jax import lax
from jax.experimental import pallas as pl
from jax.experimental.pallas import tpu as pltpu
from jax.sharding import PartitionSpec as P

norm_eps = 1e-05
MESH = pl.DeviceIdType.MESH
VMEM_SPEC = pl.BlockSpec(memory_space=pltpu.VMEM)


def round_up(value, step):
    return -(-value // step) * step


def gelu(x):
    return 0.5 * x * (1.0 + lax.erf(x * (0.5**0.5)))


def forward_kernel(
    channels, rows_at_once, x_ref, left_ref, right_ref, taps_ref, w1_ref, w2_ref, dec_ref,
    block_ref, decoded_ref, conv_ref, sum_ref, wide_ref,
):
    lon_len, padded_c, lat_len = x_ref.shape
    half = left_ref.shape[0]
    size = 2 * half + 1
    blocks = padded_c // 16
    lane = lax.broadcasted_iota(jnp.int32, (16, lat_len), 1)
    sum_ref[...] = jnp.zeros_like(sum_ref)

    def conv_block(block, carry):
        chan = pl.ds(pl.multiple_of(block * 16, 16), 16)
        for i in range(half):
            wide_ref[i] = left_ref[i, chan, :].astype(jnp.float32)
            wide_ref[half + lon_len + i] = right_ref[i, chan, :].astype(jnp.float32)
        for i in range(lon_len):
            wide_ref[half + i] = x_ref[i, chan, :].astype(jnp.float32)
        total = [None] * lon_len
        for q in range(size):
            coef = [
                jnp.broadcast_to(taps_ref[chan, p * size + q : p * size + q + 1], (16, lat_len))
                for p in range(size)
            ]
            shift = half - q
            for i in range(lon_len):
                part = coef[0] * wide_ref[i]
                for p in range(1, size):
                    part = part + coef[p] * wide_ref[i + p]
                if shift != 0:
                    part = pltpu.roll(part, shift % lat_len, 1)
                    inside = lane >= shift if shift > 0 else lane < lat_len + shift
                    part = jnp.where(inside, part, 0.0)
                if q == 0:
                    conv_ref[i, chan, :] = part
                else:
                    part = part + conv_ref[i, chan, :]
                    conv_ref[i, chan, :] = part
                if q == size - 1:
                    sum_ref[i] = sum_ref[i] + part[0:8] + part[8:16]
        return carry

    lax.fori_loop(0, blocks, conv_block, 0)

    last = padded_c - 16
    row_at = lax.broadcasted_iota(jnp.int32, (16, lat_len), 0)
    real = row_at < channels - last

    def rows_step(step, carry):
        normed_rows = []
        for r in range(rows_at_once):
            row = step * rows_at_once + r
            center = jnp.sum(sum_ref[row], axis=0, keepdims=True) * (1.0 / channels)
            head = conv_ref[row, 0:last, :] - center
            tail = jnp.where(real, conv_ref[row, last:padded_c, :] - center, 0.0)
            square = jnp.sum(head * head, axis=0, keepdims=True) + jnp.sum(
                tail * tail, axis=0, keepdims=True
            )
            scale = lax.rsqrt(square * (1.0 / channels) + norm_eps)
            normed_rows.append(
                jnp.concatenate(
                    [(head * scale).astype(jnp.bfloat16), (tail * scale).astype(jnp.bfloat16)],
                    axis=0,
                )
            )
        normed = jnp.concatenate(normed_rows, axis=1)
        hid = w1_ref.shape[0]
        piece = hid // 3
        out = None
        for k in range(3):
            pre = jnp.dot(
                w1_ref[k * piece : (k + 1) * piece, :], normed, preferred_element_type=jnp.float32
            )
            act = gelu(pre).astype(jnp.bfloat16)
            part = jnp.dot(w2_ref[k], act, preferred_element_type=jnp.float32)
            out = part if out is None else out + part
        feats = jnp.concatenate(
            [x_ref[step * rows_at_once + r] for r in range(rows_at_once)], axis=1
        ).astype(jnp.float32)
        block_out = (feats + out).astype(jnp.bfloat16)
        decoded = jnp.dot(dec_ref[...], block_out, preferred_element_type=jnp.float32).astype(
            jnp.bfloat16
        )
        for r in range(rows_at_once):
            cols = slice(r * lat_len, (r + 1) * lat_len)
            block_ref[step * rows_at_once + r] = block_out[:, cols]
            decoded_ref[step * rows_at_once + r] = decoded[:, cols]
        return carry

    lax.fori_loop(0, lon_len // rows_at_once, rows_step, 0)


def score_kernel(
    rows_at_once, scale, every_ref, own_ref, block_ref, observed_ref, weight_ref, dec_ref,
    grad_ref, term_ref,
):
    members = every_ref.shape[0]
    lon_len, outputs, lat_len = own_ref.shape
    term_ref[...] = jnp.zeros_like(term_ref)

    def rows_step(step, carry):
        score_rows = []
        for r in range(rows_at_once):
            row = step * rows_at_once + r
            own = own_ref[row].astype(jnp.float32)
            misfit = own - observed_ref[row]
            total = misfit * lax.rsqrt(jnp.sum(misfit * misfit, axis=0, keepdims=True) + 1.0)
            pair_sum = jnp.zeros_like(own)
            for k in range(members):
                apart = own - every_ref[k, row].astype(jnp.float32)
                pair_sum = pair_sum + apart * lax.rsqrt(
                    jnp.sum(apart * apart, axis=0, keepdims=True) + 1.0
                )
            weight = weight_ref[pl.ds(row, 1), :]
            score_rows.append((weight * (total - pair_sum / members)).astype(jnp.bfloat16))
        score = jnp.concatenate(score_rows, axis=1)
        block = jnp.concatenate(
            [block_ref[step * rows_at_once + r] for r in range(rows_at_once)], axis=1
        )
        grad = jnp.dot(dec_ref[...], score, preferred_element_type=jnp.float32).astype(jnp.bfloat16)
        for r in range(rows_at_once):
            grad_ref[step * rows_at_once + r] = grad[:, r * lat_len : (r + 1) * lat_len]
        term_ref[...] += scale * lax.dot_general(
            score, block, (((1,), (1,)), ((), ())), preferred_element_type=jnp.float32
        )
        return carry

    lax.fori_loop(0, lon_len // rows_at_once, rows_step, 0)


def reduce_kernel(groups, term_ref, out_ref, mine, got, own, whole, sems):
    send1, recv1, send2, recv2 = (sems.at[i] for i in range(4))
    member_n, space_n = groups
    n = member_n * space_n
    per = own.shape[0]
    me = lax.axis_index("member") * space_n + lax.axis_index("space")

    def peer(e):
        other = lax.rem(me + e + 1, n)
        return other, (other // space_n, lax.rem(other, space_n))

    barrier = pltpu.get_barrier_semaphore()

    def greet(e, carry):
        pl.semaphore_signal(barrier, inc=1, device_id=peer(e)[1], device_id_type=MESH)
        return carry

    lax.fori_loop(0, n - 1, greet, 0)
    tall = term_ref.shape[0] // 8
    across = term_ref.shape[1] // 128
    for a in range(tall):
        for b in range(across):
            at = a * across + b
            mine[at // per, at % per] = term_ref[8 * a : 8 * a + 8, 128 * b : 128 * b + 128]
    for at in range(tall * across, n * per):
        mine[at // per, at % per] = jnp.zeros((8, 128), jnp.float32)
    pl.semaphore_wait(barrier, n - 1)

    def scatter_copy(e):
        other, device = peer(e)
        return pltpu.make_async_remote_copy(
            src_ref=mine.at[other], dst_ref=got.at[e], send_sem=send1.at[e], recv_sem=recv1.at[e],
            device_id=device, device_id_type=MESH,
        )

    def gather_copy(e):
        _, device = peer(e)
        return pltpu.make_async_remote_copy(
            src_ref=own, dst_ref=whole.at[e], send_sem=send2.at[e], recv_sem=recv2.at[e],
            device_id=device, device_id_type=MESH,
        )

    def start(make):
        def body(e, carry):
            make(e).start()
            return carry

        lax.fori_loop(0, n - 1, body, 0)

    def finish(make):
        def body(e, carry):
            make(e).wait()
            return carry

        lax.fori_loop(0, n - 1, body, 0)

    start(scatter_copy)
    finish(scatter_copy)
    total = mine[me]
    for e in range(n - 1):
        total = total + got[e]
    own[...] = total
    start(gather_copy)
    out_ref[me] = total
    finish(gather_copy)
    for e in range(n - 1):
        out_ref[lax.rem(me + n - e - 1, n)] = whole[e]


def per_device(features, depth_kernel, in_weight, out_weight, decoder_weight, observed, land_mask):
    _, channels, lon_len, lat_len = features.shape
    hid = in_weight.shape[1]
    outputs = decoder_weight.shape[1]
    size = depth_kernel.shape[1]
    half = size // 2
    member_n = lax.axis_size("member")
    space_n = lax.axis_size("space")
    n = member_n * space_n
    members = features.shape[0] * member_n
    total_points = lon_len * space_n * lat_len
    padded_c = round_up(channels, 16)
    padded_h = round_up(hid, 48)
    more_c = padded_c - channels
    more_h = padded_h - hid

    x = jnp.pad(jnp.transpose(features[0], (1, 0, 2)), ((0, 0), (0, more_c), (0, 0)))
    forth = [(i, (i + 1) % space_n) for i in range(space_n)]
    back = [((i + 1) % space_n, i) for i in range(space_n)]
    left = lax.ppermute(x[lon_len - half :], "space", forth)
    right = lax.ppermute(x[:half], "space", back)
    taps = jnp.pad(depth_kernel.reshape(channels, size * size), ((0, more_c), (0, 0)))
    w1 = jnp.pad(in_weight.T, ((0, more_h), (0, more_c)))
    w2 = jnp.pad(out_weight.T, ((0, more_c), (0, more_h)))
    w2 = jnp.stack(jnp.split(w2, 3, axis=1))
    dec_t = jnp.pad(decoder_weight.T, ((0, 0), (0, more_c)))
    block_out, decoded = pl.pallas_call(
        functools.partial(forward_kernel, channels, 2),
        name="forward",
        out_shape=(
            jax.ShapeDtypeStruct((lon_len, padded_c, lat_len), jnp.bfloat16),
            jax.ShapeDtypeStruct((lon_len, outputs, lat_len), jnp.bfloat16),
        ),
        in_specs=[VMEM_SPEC] * 7,
        out_specs=[VMEM_SPEC] * 2,
        scratch_shapes=[
            pltpu.VMEM((lon_len, padded_c, lat_len), jnp.float32),
            pltpu.VMEM((lon_len, 8, lat_len), jnp.float32),
            pltpu.VMEM((lon_len + 2 * half, 16, lat_len), jnp.float32),
        ],
    )(x, left, right, taps, w1, w2, dec_t)
    every = lax.all_gather(decoded, "member", axis=0)
    weight = 4.0 + 8.0 * land_mask.astype(jnp.float32)
    grad, term = pl.pallas_call(
        functools.partial(score_kernel, 2, 1.0 / math.sqrt(members * total_points)),
        name="score",
        out_shape=(
            jax.ShapeDtypeStruct((lon_len, channels, lat_len), jnp.bfloat16),
            jax.ShapeDtypeStruct((outputs, padded_c), jnp.float32),
        ),
        in_specs=[VMEM_SPEC] * 6,
        out_specs=[VMEM_SPEC] * 2,
    )(every, decoded, block_out, jnp.transpose(observed, (1, 0, 2)), weight, decoder_weight)
    wide_c = round_up(padded_c, 128)
    tiles = (outputs // 8) * (wide_c // 128)
    per = -(-tiles // n)
    summed = pl.pallas_call(
        functools.partial(reduce_kernel, (member_n, space_n)),
        name="reduce",
        out_shape=jax.ShapeDtypeStruct((n, per, 8, 128), jnp.float32),
        in_specs=[VMEM_SPEC],
        out_specs=VMEM_SPEC,
        scratch_shapes=[
            pltpu.VMEM((n, per, 8, 128), jnp.float32),
            pltpu.VMEM((n - 1, per, 8, 128), jnp.float32),
            pltpu.VMEM((per, 8, 128), jnp.float32),
            pltpu.VMEM((n - 1, per, 8, 128), jnp.float32),
            pltpu.SemaphoreType.DMA((4, n - 1)),
        ],
        compiler_params=pltpu.CompilerParams(collective_id=0, has_side_effects=True),
    )(jnp.pad(term, ((0, 0), (0, wide_c - padded_c))))
    flat = summed.reshape(n * per, 8, 128)[:tiles].reshape(outputs // 8, wide_c // 128, 8, 128)
    decoder_grad = jnp.transpose(flat, (0, 2, 1, 3)).reshape(outputs, wide_c)[:, :channels].T
    grad_features = jnp.transpose(grad, (1, 0, 2))[None]
    return (grad_features, decoder_grad)


def solution(mesh):
    placed = (
        P("member", None, "space", None),
        P(),
        P(),
        P(),
        P(),
        P(None, "space", None),
        P("space", None),
    )
    return jax.shard_map(
        per_device,
        mesh=mesh,
        in_specs=placed,
        out_specs=(P("member", None, "space", None), P()),
        check_vma=False,
    )
```

time: 393 us -> 153 us (0.39)
  other arithmetic: 150 us -> 2.18 us
  waiting for transfers between devices: 144 us -> 20.5 us
  Pallas kernels: 0 us -> 86.7 us
  matrix products: 56.1 us -> 0 us
    reduce_sum x5 -> x0, other arithmetic: 139 us -> none  [the longest x1 131 us: per_device(): center = jnp.mean(convolved, axis=1, keepdims=True)]
    psum x1 -> x0, waiting for transfers between devices: 119 us -> none  [per_device(): decoder_grad = lax.psum(term, ('member', 'space'))]
    pallas_call x0 -> x3, Pallas kernels: none -> 86.7 us  [the longest x1 53.3 us: per_device(): pl.pallas_call(functools.partial(forward_kernel, channels, 2), name='forw...]
    dot_general x5 -> x0, matrix products: 56.1 us -> none  [the longest x1 42.9 us: per_device(): jnp.einsum('ch,cp->hp', in_weight, flat, preferred_element_type=jnp.float32)]
    convert_element_type x2 -> x0, other arithmetic: 7.07 us -> none  [the longest x1 6.87 us: per_device(): padded.astype(jnp.float32)]
    pad x0 -> x5, local copies, waits for them, and re-layouts: none -> 5.86 us  [the longest x1 2.19 us: per_device(): jnp.pad(jnp.transpose(features[0], (1, 0, 2)), ((0, 0), (0, more_c), (0,...]
    unnamed x36 -> x19, local copies, waits for them, and re-layouts: 16.6 us -> 12.8 us
  transfers between devices with their start and end apart: 4 -> 3, of which waited for: 4 -> 2; matrix products, arithmetic and copies ran while one was open for 4% -> 10% of each run, Pallas kernels for 0% -> 0%
where the time goes in v1:
time: 153 us; the launch traced here: 152 us
  Pallas kernels  86.7 us (57%)
  local copies, waits for them, and re-layouts  22.8 us (15%)
  waiting for transfers between devices  20.5 us (13%)
  between operations  14.1 us (9%)
  starting transfers between devices  6.19 us (4%)
  other arithmetic  2.18 us (1%)
    pallas_call x1, Pallas kernels, per_device(): pl.pallas_call(functools.partial(forward_kernel, channels, 2), name='forw...  53.3 us
    pallas_call x1, Pallas kernels, per_device(): pl.pallas_call(functools.partial(reduce_kernel, (member_n, space_n)), nam...  23.4 us
    all_gather x1, waiting for transfers between devices, per_device(): every = lax.all_gather(decoded, 'member', axis=0)  19.2 us
    unnamed x19, local copies, waits for them, and re-layouts  12.8 us
    pallas_call x1, Pallas kernels, per_device(): pl.pallas_call(functools.partial(score_kernel, 2, 1.0 / math.sqrt(members...  9.99 us
    ppermute x1, starting transfers between devices, per_device(): right = lax.ppermute(x[:half], 'space', back)  3.1 us
  transfers between devices with their start and end apart: 3, of which 2 were waited for; matrix products, arithmetic and copies ran while one was open for 10% of the time, Pallas kernels for 0%

profile of v1, /device:TPU:0, one launch (start us, length us, event | category | flops | bytes accessed | tf_op | source)
XLA Modules:
  0.0 152.4 jit_solution(7327701457237791732)
XLA Ops:
  7.2 0.0 all-gather.3.cloned.1.call-start
  7.2 2.6 %copy.29 = bf16[1,641,24,128]{3,1,2,0:T(8,128)(2,1)S(1)} copy(bf16[1,641,24,128]{3,2,1,0:T(8,128)(2,1)} %param.7) | data formatting | bytes 7876608 | tf_op args[0]
  9.9 3.0 %collective-permute-start = (bf16[2,656,128]{2,1,0:T(8,128)(2,1)S(1)}, bf16[2,656,128]{2,1,0:T(8,128)(2,1)S(1)}, u32[]{:S(2)}, u32[]{:S(2)}) collective-permute-start(bf16[2,656,128]{2,1,0:T(8,128)(2,1)S(1)} %get-tuple-element.17), channel_id=1, source_target_pairs={{0,1},{1,2},{2,3},{3,4},{4,5},{5,6},{6,7},{7,0},{8,9},{9,10},{10,1... | collective-permute-start | bytes 1007624 | tf_op jit(solution)/shard_map/ppermute | solution.py:242
  12.9 3.1 %collective-permute-start.1 = (bf16[2,656,128]{2,1,0:T(8,128)(2,1)S(1)}, bf16[2,656,128]{2,1,0:T(8,128)(2,1)S(1)}, u32[]{:S(2)}, u32[]{:S(2)}) collective-permute-start(bf16[2,656,128]{2,1,0:T(8,128)(2,1)S(1)} %get-tuple-element.16), channel_id=1, source_target_pairs={{1,0},{2,1},{3,2},{4,3},{5,4},{6,5},{7,6},{0,7},{9,8},{10,9},{11,1... | collective-permute-start | bytes 1007624 | tf_op jit(solution)/shard_map/ppermute | solution.py:243
  16.1 2.2 %pad.24.x_ref = bf16[24,656,128]{2,1,0:T(8,128)(2,1)} pad(bf16[24,641,128]{2,1,0:T(8,128)(2,1)S(1)} %bitcast.31, bf16[]{:T(256)} %constant.2.clone.1), padding=0_0x0_15x0_0 | pad | bytes 7968770 | tf_op jit(solution)/shard_map/jit(_pad)/pad | solution.py:239
  18.2 2.9 %copy.23 = bf16[641,1282]{0,1:T(8,128)(2,1)S(1)} copy(bf16[641,1282]{1,0:T(8,128)(2,1)} %param.9) | data formatting | bytes 3287048 | tf_op args[2]
  21.2 0.0 copy-start.5
  21.2 0.0 copy-start.1
  21.2 1.6 %pad.26.w1_ref = bf16[1296,656]{1,0:T(8,128)(2,1)} pad(bf16[1282,641]{1,0:T(8,128)(2,1)S(1)} %bitcast.32, bf16[]{:T(256)} %constant.2.clone.1), padding=0_14x0_15 | pad | bytes 3343878 | tf_op jit(solution)/shard_map/jit(_pad)/pad | solution.py:245
  22.8 0.0 copy-done.5
  22.8 0.2 copy.22
  23.0 0.0 copy-done.1
  23.0 0.7 pad.28.dec_ref
  23.6 0.7 pad.25.taps_ref
  24.4 2.2 %fusion = (bf16[1,656,432]{2,1,0:T(8,128)(2,1)S(1)}, bf16[1,656,432]{2,1,0:T(8,128)(2,1)S(1)}, bf16[1,656,432]{2,1,0:T(8,128)(2,1)S(1)}) fusion(bf16[641,1282]{1,0:T(8,128)(2,1)} %bitcast.35), kind=kLoop, calls=%fused_computation.6 | loop fusion | bytes 3343876 | tf_op jit(solution)/shard_map/stack | solution.py:247
  26.6 1.6 %pad_maximum_fusion.w2_ref = bf16[3,656,432]{2,1,0:T(8,128)(2,1)} fusion(bf16[1,656,432]{2,1,0:T(8,128)(2,1)S(1)} %get-tuple-element.20, bf16[1,656,432]{2,1,0:T(8,128)(2,1)S(1)} %get-tuple-element.19, bf16[1,656,432]{2,1,0:T(8,128)(2,1)S(1)} %get-tuple-element.18), kind=kLoop, calls=%fused_computation.1 | loop fusion | flops 1700352 | bytes 3400704 | tf_op jit(solution)/shard_map/stack | solution.py:247
  28.2 0.0 copy-start
  28.2 0.0 collective-permute-done.left_ref
  28.2 0.0 copy-start.2
  28.2 1.3 collective-permute-done.1.right_ref
  29.5 0.0 copy-done.2
  29.5 0.0 copy-start.3
  29.5 0.8 copy-done.3
  30.2 53.3 %forward.1 = (bf16[24,656,128]{2,1,0:T(8,128)(2,1)}, bf16[24,72,128]{2,1,0:T(8,128)(2,1)}) custom-call(bf16[24,656,128]{2,1,0:T(8,128)(2,1)} %pad.24.x_ref, bf16[2,656,128]{2,1,0:T(8,128)(2,1)} %copy-done.2, bf16[2,656,128]{2,1,0:T(8,128)(2,1)} %copy-done.3, f32[656,25]{1,0:T(8,128)} %pad.25.taps_ref, bf16[1296,656]{1,0:T(8,128)(2,1)} %pad.26.w1_ref, ...), custom_call_target="tpu_custom_call" | custom-call | tf_op jit(solution)/shard_map/forward/pallas_call | solution.py:249
  83.6 0.0 copy-start.6
  83.6 0.0 all-gather.3.cloned.1.call-update
  83.6 0.8 copy.25.dec_ref
  84.4 0.0 copy-done
  84.4 1.1 copy.30
  85.5 0.0 copy-done.6
  85.5 0.6 multiply_add_fusion.weight_ref
  86.1 19.2 %all-gather.3.cloned.1.call-done = bf16[96,72,128]{2,1,0:T(8,128)(2,1)} async-done(((bf16[24,72,128]{2,1,0:T(8,128)(2,1)}), bf16[96,72,128]{2,1,0:T(8,128)(2,1)}) %all-gather.3.cloned.1.call-update) | async-done | bytes 1769488 | tf_op jit(solution)/shard_map/all_gather | solution.py:264
  105.3 10.0 %score.1 = (bf16[24,641,128]{2,1,0:T(8,128)(2,1)}, f32[72,656]{1,0:T(8,128)}) custom-call(bf16[4,24,72,128]{3,2,1,0:T(8,128)(2,1)} %bitcast.36, bf16[24,72,128]{2,1,0:T(8,128)(2,1)} %get-tuple-element.6.own_ref, bf16[24,656,128]{2,1,0:T(8,128)(2,1)} %get-tuple-element.7.block_ref, f32[24,72,128]{2,1,0:T(8,128)} %bitcast.34, ...), custom_call_target="tpu_custom_call" | custom-call | tf_op jit(solution)/shard_map/score/pallas_call | solution.py:266
  115.2 0.0 copy-start.4
  115.2 4.6 %copy.26 = bf16[1,641,24,128]{3,2,1,0:T(8,128)(2,1)} copy(bf16[1,641,24,128]{3,1,2,0:T(8,128)(2,1)} %bitcast.33) | data formatting | bytes 7876608
  119.8 0.0 copy-done.4
  119.9 0.7 pad.29.term_ref
  120.6 23.4 %reduce.1 = f32[32,2,8,128]{3,2,1,0:T(8,128)} custom-call(f32[72,768]{1,0:T(8,128)} %pad.29.term_ref), custom_call_target="tpu_custom_call" | custom-call | tf_op jit(solution)/shard_map/reduce/pallas_call | solution.py:279
  143.9 1.0 slice.15
  144.9 0.7 slice_bitcast_fusion
  (2 shorter events, 0.1 us)
Async XLA Ops:
  7.2 98.1 %all-gather.3.cloned.1.call-start = ((), (), s32[]{:S(2)}) async-start(), calls=%async_computation | async-start | bytes 2211840 | tf_op jit(solution)/shard_map/all_gather | solution.py:264
  9.9 18.3 %collective-permute-start = (bf16[2,656,128]{2,1,0:T(8,128)(2,1)S(1)}, bf16[2,656,128]{2,1,0:T(8,128)(2,1)S(1)}, u32[]{:S(2)}, u32[]{:S(2)}) collective-permute-start(bf16[2,656,128]{2,1,0:T(8,128)(2,1)S(1)} %get-tuple-element.17), channel_id=1, source_target_pairs={{0,1},{1,2},{2,3},{3,4},{4,5},{5,6},{6,7},{7,0},{8,9},{9,10},{10,1... | collective-permute-start | bytes 1007624 | tf_op jit(solution)/shard_map/ppermute | solution.py:242
  12.9 16.5 %collective-permute-start.1 = (bf16[2,656,128]{2,1,0:T(8,128)(2,1)S(1)}, bf16[2,656,128]{2,1,0:T(8,128)(2,1)S(1)}, u32[]{:S(2)}, u32[]{:S(2)}) collective-permute-start(bf16[2,656,128]{2,1,0:T(8,128)(2,1)S(1)} %get-tuple-element.16), channel_id=1, source_target_pairs={{1,0},{2,1},{3,2},{4,3},{5,4},{6,5},{7,6},{0,7},{9,8},{10,9},{11,1... | collective-permute-start | bytes 1007624 | tf_op jit(solution)/shard_map/ppermute | solution.py:243
  21.2 1.6 %copy-start.5 = (f32[641,5,5]{0,2,1:T(8,128)S(1)}, f32[641,5,5]{0,2,1:T(8,128)}, u32[]{:S(2)}) copy-start(f32[641,5,5]{0,2,1:T(8,128)} %param.8) | copy-start | bytes 192304
  21.2 1.8 %copy-start.1 = (bf16[641,72]{0,1:T(8,128)(2,1)S(1)}, bf16[641,72]{0,1:T(8,128)(2,1)}, u32[]{:S(2)}) copy-start(bf16[641,72]{0,1:T(8,128)(2,1)} %param.11) | copy-start | bytes 276916
  28.2 56.2 %copy-start = (f32[72,24,128]{2,1,0:T(8,128)S(1)}, f32[72,24,128]{2,1,0:T(8,128)}, u32[]{:S(2)}) copy-start(f32[72,24,128]{2,1,0:T(8,128)} %param.12) | copy-start | bytes 2654212
  28.2 1.3 copy-start.2
  29.5 0.8 copy-start.3
  83.6 1.9 %copy-start.6 = (s32[24,128]{1,0:T(8,128)S(1)}, s32[24,128]{1,0:T(8,128)}, u32[]{:S(2)}) copy-start(s32[24,128]{1,0:T(8,128)} %param.13) | copy-start | bytes 36868
  115.2 4.6 %copy-start.4 = (f32[72,656]{1,0:T(8,128)S(1)}, f32[72,656]{1,0:T(8,128)}, u32[]{:S(2)}) copy-start(f32[72,656]{1,0:T(8,128)} %get-tuple-element.9) | copy-start | bytes 566788
Sparse Core Ops, SparseCore 0:
  83.7 21.4 all-gather.2

commit v2 on v1

v2 whole, which is shorter than its diff:
```python
import functools
import math

import jax
import jax.numpy as jnp
from jax import lax
from jax.experimental import pallas as pl
from jax.experimental.pallas import tpu as pltpu
from jax.sharding import PartitionSpec as P

norm_eps = 1e-05
MESH = pl.DeviceIdType.MESH
VMEM_SPEC = pl.BlockSpec(memory_space=pltpu.VMEM)


def round_up(value, step):
    return -(-value // step) * step


def gelu(x):
    return 0.5 * x * (1.0 + lax.erf(x * (0.5**0.5)))


def conv_kernel(x_ref, left_ref, right_ref, taps_ref, normed_ref, conv_ref, sum_ref, wide_ref):
    lon_len, channels, lat_len = x_ref.shape
    half = left_ref.shape[0]
    size = 2 * half + 1
    full = channels // 16
    rest = channels - full * 16
    lane = lax.broadcasted_iota(jnp.int32, (16, lat_len), 1)
    sum_ref[...] = jnp.zeros_like(sum_ref)

    def convolve(chan):
        for q in range(size):
            coef = [
                jnp.broadcast_to(taps_ref[chan, p * size + q : p * size + q + 1], (16, lat_len))
                for p in range(size)
            ]
            shift = half - q
            for i in range(lon_len):
                part = coef[0] * wide_ref[i]
                for p in range(1, size):
                    part = part + coef[p] * wide_ref[i + p]
                if shift != 0:
                    part = pltpu.roll(part, shift % lat_len, 1)
                    inside = lane >= shift if shift > 0 else lane < lat_len + shift
                    part = jnp.where(inside, part, 0.0)
                if q > 0:
                    part = part + conv_ref[i, chan, :]
                conv_ref[i, chan, :] = part
                if q == size - 1:
                    sum_ref[i] = sum_ref[i] + part[0:8] + part[8:16]

    def conv_block(block, carry):
        chan = pl.ds(pl.multiple_of(block * 16, 16), 16)
        for i in range(half):
            wide_ref[i] = left_ref[i, chan, :].astype(jnp.float32)
            wide_ref[half + lon_len + i] = right_ref[i, chan, :].astype(jnp.float32)
        for i in range(lon_len):
            wide_ref[half + i] = x_ref[i, chan, :].astype(jnp.float32)
        convolve(chan)
        return carry

    lax.fori_loop(0, full, conv_block, 0)
    if rest > 0:
        wide_ref[...] = jnp.zeros_like(wide_ref)
        for i in range(half):
            wide_ref[i, 0:rest, :] = left_ref[i, full * 16 : channels, :].astype(jnp.float32)
            wide_ref[half + lon_len + i, 0:rest, :] = right_ref[i, full * 16 : channels, :].astype(
                jnp.float32
            )
        for i in range(lon_len):
            wide_ref[half + i, 0:rest, :] = x_ref[i, full * 16 : channels, :].astype(jnp.float32)
        convolve(slice(full * 16, full * 16 + 16))

    def norm_row(row, carry):
        center = jnp.sum(sum_ref[row], axis=0, keepdims=True) * (1.0 / channels)
        shifted = conv_ref[row, 0:channels, :] - center
        square = jnp.sum(shifted * shifted, axis=0, keepdims=True)
        scale = lax.rsqrt(square * (1.0 / channels) + norm_eps)
        normed_ref[row] = (shifted * scale).astype(jnp.bfloat16)
        return carry

    lax.fori_loop(0, lon_len, norm_row, 0)


def cuts_of(hid):
    width = round_up(-(-hid // 3), 256)
    return [(at, min(at + width, hid)) for at in range(0, hid, width)]


def main_kernel(
    groups, rows_at_once, scale, x_ref, normed_ref, w1_ref, w2_ref, dect_ref, dec_ref, observed_ref,
    weight_ref, grad_ref, out_ref, block_ref, own_ref, others_ref, score_ref, term_ref, mine, got,
    mine_sum, whole, pair_sems, sems,
):
    lon_len, channels, lat_len = x_ref.shape
    member_n, space_n = groups
    n = member_n * space_n
    member = lax.axis_index("member")
    space = lax.axis_index("space")
    me = member * space_n + space
    steps = lon_len // rows_at_once

    def peer(e):
        other = lax.rem(me + e + 1, n)
        return other, (other // space_n, lax.rem(other, space_n))

    barrier = pltpu.get_barrier_semaphore()

    def greet(e, carry):
        pl.semaphore_signal(barrier, inc=1, device_id=peer(e)[1], device_id_type=MESH)
        return carry

    lax.fori_loop(0, n - 1, greet, 0)

    def joined(ref, step):
        return jnp.concatenate([ref[step * rows_at_once + r] for r in range(rows_at_once)], axis=1)

    def mlp_step(step):
        normed = joined(normed_ref, step)
        out = joined(x_ref, step).astype(jnp.float32)
        for low, high in cuts_of(w1_ref.shape[0]):
            pre = jnp.dot(w1_ref[low:high, :], normed, preferred_element_type=jnp.float32)
            act = gelu(pre).astype(jnp.bfloat16)
            out = out + jnp.dot(w2_ref[:, low:high], act, preferred_element_type=jnp.float32)
        block_out = out.astype(jnp.bfloat16)
        decoded = jnp.dot(dect_ref[...], block_out, preferred_element_type=jnp.float32).astype(
            jnp.bfloat16
        )
        for r in range(rows_at_once):
            cols = slice(r * lat_len, (r + 1) * lat_len)
            block_ref[step * rows_at_once + r] = block_out[:, cols]
            own_ref[step * rows_at_once + r] = decoded[:, cols]

    def pair_copy(step, j):
        rows = pl.ds(step * rows_at_once, rows_at_once)
        return pltpu.make_async_remote_copy(
            src_ref=own_ref.at[rows], dst_ref=others_ref.at[j, rows],
            send_sem=pair_sems.at[0, j, step], recv_sem=pair_sems.at[1, j, step],
            device_id=(lax.rem(member + j + 1, member_n), space), device_id_type=MESH,
        )

    mlp_step(0)
    pl.semaphore_wait(barrier, n - 1)
    for j in range(member_n - 1):
        pair_copy(0, j).start()

    def mlp_loop(step, carry):
        mlp_step(step)
        for j in range(member_n - 1):
            pair_copy(step, j).start()
        return carry

    lax.fori_loop(1, steps, mlp_loop, 0)
    term_ref[...] = jnp.zeros_like(term_ref)

    def score_step(step, carry):
        for j in range(member_n - 1):
            pair_copy(step, j).wait()
        for r in range(rows_at_once):
            row = step * rows_at_once + r
            own = own_ref[row].astype(jnp.float32)
            misfit = own - observed_ref[row]
            total = misfit * lax.rsqrt(jnp.sum(misfit * misfit, axis=0, keepdims=True) + 1.0)
            pair_sum = jnp.zeros_like(own)
            for k in range(member_n):
                other = own_ref[row] if k == member_n - 1 else others_ref[k, row]
                apart = own - other.astype(jnp.float32)
                pair_sum = pair_sum + apart * lax.rsqrt(
                    jnp.sum(apart * apart, axis=0, keepdims=True) + 1.0
                )
            weight = weight_ref[pl.ds(row, 1), :]
            score_ref[row] = (weight * (total - pair_sum / member_n)).astype(jnp.bfloat16)
        term_ref[:, 0:channels] += lax.dot_general(
            joined(score_ref, step), joined(block_ref, step), (((1,), (1,)), ((), ())),
            preferred_element_type=jnp.float32,
        )
        return carry

    lax.fori_loop(0, steps, score_step, 0)

    def grad_step(step, carry):
        grad = jnp.dot(
            dec_ref[...], joined(score_ref, step), preferred_element_type=jnp.float32
        ).astype(jnp.bfloat16)
        for r in range(rows_at_once):
            grad_ref[step * rows_at_once + r] = grad[:, r * lat_len : (r + 1) * lat_len]
        return carry

    per = mine_sum.shape[0]
    tall = term_ref.shape[0] // 8
    across = term_ref.shape[1] // 128
    for a in range(tall):
        for b in range(across):
            at = a * across + b
            mine[at // per, at % per] = (
                scale * term_ref[8 * a : 8 * a + 8, 128 * b : 128 * b + 128]
            )
    for at in range(tall * across, n * per):
        mine[at // per, at % per] = jnp.zeros((8, 128), jnp.float32)

    def scatter_copy(e):
        other, device = peer(e)
        return pltpu.make_async_remote_copy(
            src_ref=mine.at[other], dst_ref=got.at[e], send_sem=sems.at[0, e],
            recv_sem=sems.at[1, e], device_id=device, device_id_type=MESH,
        )

    def gather_copy(e):
        _, device = peer(e)
        return pltpu.make_async_remote_copy(
            src_ref=mine_sum, dst_ref=whole.at[e], send_sem=sems.at[2, e],
            recv_sem=sems.at[3, e], device_id=device, device_id_type=MESH,
        )

    def start(make):
        def body(e, carry):
            make(e).start()
            return carry

        lax.fori_loop(0, n - 1, body, 0)

    def finish(make):
        def body(e, carry):
            make(e).wait()
            return carry

        lax.fori_loop(0, n - 1, body, 0)

    start(scatter_copy)
    lax.fori_loop(0, steps // 2, grad_step, 0)
    finish(scatter_copy)
    total = mine[me]
    for e in range(n - 1):
        total = total + got[e]
    mine_sum[...] = total
    start(gather_copy)
    out_ref[me] = total
    lax.fori_loop(steps // 2, steps, grad_step, 0)
    finish(gather_copy)
    for e in range(n - 1):
        out_ref[lax.rem(me + n - e - 1, n)] = whole[e]


def per_device(features, depth_kernel, in_weight, out_weight, decoder_weight, observed, land_mask):
    _, channels, lon_len, lat_len = features.shape
    outputs = decoder_weight.shape[1]
    size = depth_kernel.shape[1]
    half = size // 2
    member_n = lax.axis_size("member")
    space_n = lax.axis_size("space")
    n = member_n * space_n
    members = features.shape[0] * member_n
    total_points = lon_len * space_n * lat_len
    padded_c = round_up(channels, 16)

    x = jnp.transpose(features[0], (1, 0, 2))
    forth = [(i, (i + 1) % space_n) for i in range(space_n)]
    back = [((i + 1) % space_n, i) for i in range(space_n)]
    left = lax.ppermute(x[lon_len - half :], "space", forth)
    right = lax.ppermute(x[:half], "space", back)
    taps = jnp.pad(depth_kernel.reshape(channels, size * size), ((0, padded_c - channels), (0, 0)))
    normed = pl.pallas_call(
        conv_kernel,
        name="conv",
        out_shape=jax.ShapeDtypeStruct((lon_len, channels, lat_len), jnp.bfloat16),
        in_specs=[VMEM_SPEC] * 4,
        out_specs=VMEM_SPEC,
        scratch_shapes=[
            pltpu.VMEM((lon_len, padded_c, lat_len), jnp.float32),
            pltpu.VMEM((lon_len, 8, lat_len), jnp.float32),
            pltpu.VMEM((lon_len + 2 * half, 16, lat_len), jnp.float32),
        ],
    )(x, left, right, taps)
    weight = 4.0 + 8.0 * land_mask.astype(jnp.float32)
    wide_c = round_up(channels, 128)
    tiles = (outputs // 8) * (wide_c // 128)
    per = -(-tiles // n)
    rows_at_once = 2
    grad, summed = pl.pallas_call(
        functools.partial(
            main_kernel, (member_n, space_n), rows_at_once, 1.0 / math.sqrt(members * total_points)
        ),
        name="main",
        out_shape=(
            jax.ShapeDtypeStruct((lon_len, channels, lat_len), jnp.bfloat16),
            jax.ShapeDtypeStruct((n, per, 8, 128), jnp.float32),
        ),
        in_specs=[VMEM_SPEC] * 8,
        out_specs=[VMEM_SPEC] * 2,
        scratch_shapes=[
            pltpu.VMEM((lon_len, channels, lat_len), jnp.bfloat16),
            pltpu.VMEM((lon_len, outputs, lat_len), jnp.bfloat16),
            pltpu.VMEM((member_n - 1, lon_len, outputs, lat_len), jnp.bfloat16),
            pltpu.VMEM((lon_len, outputs, lat_len), jnp.bfloat16),
            pltpu.VMEM((outputs, wide_c), jnp.float32),
            pltpu.VMEM((n, per, 8, 128), jnp.float32),
            pltpu.VMEM((n - 1, per, 8, 128), jnp.float32),
            pltpu.VMEM((per, 8, 128), jnp.float32),
            pltpu.VMEM((n - 1, per, 8, 128), jnp.float32),
            pltpu.SemaphoreType.DMA((2, member_n - 1, lon_len // rows_at_once)),
            pltpu.SemaphoreType.DMA((4, n - 1)),
        ],
        compiler_params=pltpu.CompilerParams(collective_id=0, has_side_effects=True),
    )(
        x, normed, in_weight.T, out_weight.T, decoder_weight.T, decoder_weight,
        jnp.transpose(observed, (1, 0, 2)), weight,
    )
    flat = summed.reshape(n * per, 8, 128)[:tiles].reshape(outputs // 8, wide_c // 128, 8, 128)
    decoder_grad = jnp.transpose(flat, (0, 2, 1, 3)).reshape(outputs, wide_c)[:, :channels].T
    grad_features = jnp.transpose(grad, (1, 0, 2))[None]
    return (grad_features, decoder_grad)


def solution(mesh):
    placed = (
        P("member", None, "space", None),
        P(),
        P(),
        P(),
        P(),
        P(None, "space", None),
        P("space", None),
    )
    return jax.shard_map(
        per_device,
        mesh=mesh,
        in_specs=placed,
        out_specs=(P("member", None, "space", None), P()),
        check_vma=False,
    )
```

time: 153 us -> 116 us (0.76)
  waiting for transfers between devices: 20.5 us -> 6.42 us
  between operations: 14.1 us -> 0.72 us
  local copies, waits for them, and re-layouts: 22.8 us -> 16.2 us
  other arithmetic: 2.18 us -> 0.61 us
    all_gather x1 -> x0, waiting for transfers between devices: 19.2 us -> none  [per_device(): every = lax.all_gather(decoded, 'member', axis=0)]
    pad x5 -> x1, local copies, waits for them, and re-layouts: 5.86 us -> 0.8 us  [per_device(): jnp.pad(depth_kernel.reshape(channels, size * size), ((0, padded_c - chan...]
    ppermute x1, waiting for transfers between devices: 0.01 us -> 4.97 us  [per_device(): left = lax.ppermute(x[lon_len - half:], 'space', forth)]
    ppermute x1, starting transfers between devices: 3.05 us -> 0.01 us  [per_device(): left = lax.ppermute(x[lon_len - half:], 'space', forth)]
    ppermute x1, starting transfers between devices: 3.1 us -> 6.03 us  [per_device(): right = lax.ppermute(x[:half], 'space', back)]
    another operation x1 -> x0, local copies, waits for them, and re-layouts: 2.23 us -> none  [per_device(): w2 = jnp.stack(jnp.split(w2, 3, axis=1))]
    another operation x1 -> x0, other arithmetic: 1.58 us -> none  [per_device(): w2 = jnp.stack(jnp.split(w2, 3, axis=1))]
    pallas_call x3 -> x2, Pallas kernels: 86.7 us -> 86.2 us  [the longest x1 53.8 us: per_device(): pl.pallas_call(functools.partial(main_kernel, (member_n, space_n), rows_a...]
  transfers between devices with their start and end apart: 3 -> 2, of which waited for: 2 -> 2; matrix products, arithmetic and copies ran while one was open for 10% -> 5% of each run, Pallas kernels for 0% -> 0%
where the time goes in v2:
time: 116 us
  Pallas kernels  86.2 us (74%)
  local copies, waits for them, and re-layouts  16.2 us (14%)
  waiting for transfers between devices  6.42 us (6%)
  starting transfers between devices  6.04 us (5%)
    pallas_call x1, Pallas kernels, per_device(): pl.pallas_call(functools.partial(main_kernel, (member_n, space_n), rows_a...  53.8 us
    pallas_call x1, Pallas kernels, per_device(): pl.pallas_call(conv_kernel, name='conv', out_shape=jax.ShapeDtypeStruct((...  32.4 us
    unnamed x19, local copies, waits for them, and re-layouts  13.6 us
    ppermute x1, starting transfers between devices, per_device(): right = lax.ppermute(x[:half], 'space', back)  6.03 us
    ppermute x1, waiting for transfers between devices, per_device(): left = lax.ppermute(x[lon_len - half:], 'space', forth)  4.97 us
  transfers between devices with their start and end apart: 2, of which 2 were waited for; matrix products, arithmetic and copies ran while one was open for 5% of the time, Pallas kernels for 0%

profile of v2, /device:TPU:0, one launch (start us, length us, event | category | flops | bytes accessed | tf_op | source)
XLA Modules:
  0.0 116.2 jit_solution(17892814814906009971)
XLA Ops:
  0.6 0.0 copy-start.5
  0.6 0.0 copy-start.3
  0.7 0.0 copy-start.2
  0.7 2.7 %copy.23 = bf16[1,641,24,128]{3,1,2,0:T(8,128)(2,1)S(1)} copy(bf16[1,641,24,128]{3,2,1,0:T(8,128)(2,1)} %param.7) | data formatting | bytes 7876608 | tf_op args[0]
  3.4 0.0 copy-start
  3.4 0.0 copy-start.1
  3.4 2.0 %copy-done = bf16[1,641,24,128]{3,1,2,0:T(8,128)(2,1)} copy-done((bf16[1,641,24,128]{3,1,2,0:T(8,128)(2,1)}, bf16[1,641,24,128]{3,1,2,0:T(8,128)(2,1)S(1)}, u32[]{:S(2)}) %copy-start) | copy-done | bytes 3938328
  5.4 0.0 copy-start.6
  5.4 0.9 fusion
  6.3 6.0 %collective-permute-start.1 = (bf16[2,641,128]{2,1,0:T(8,128)(2,1)}, bf16[2,641,128]{2,1,0:T(8,128)(2,1)}, u32[]{:S(2)}, u32[]{:S(2)}) collective-permute-start(bf16[2,641,128]{2,1,0:T(8,128)(2,1)} %get-tuple-element.10), channel_id=1, source_target_pairs={{1,0},{2,1},{3,2},{4,3},{5,4},{6,5},{7,6},{0,7},{9,8},{10,9},{11,1... | collective-permute-start | bytes 984584 | tf_op jit(solution)/shard_map/ppermute | solution.py:262
  12.3 0.0 collective-permute-start
  12.3 0.0 copy-done.5
  12.4 0.0 copy-done.3
  12.4 0.8 copy.19.dec_ref
  13.2 0.2 copy.16
  13.3 0.0 copy-done.2
  13.4 1.1 copy.24
  14.4 0.0 copy-done.1
  14.4 2.4 %copy.17 = bf16[641,1282]{0,1:T(8,128)(2,1)} copy(bf16[641,1282]{1,0:T(8,128)(2,1)S(1)} %copy-done.1) | data formatting | bytes 3287048 | tf_op args[2]
  16.8 0.8 pad.4.taps_ref
  17.6 0.0 copy-done.6
  17.6 0.6 multiply_add_fusion.weight_ref
  18.3 1.5 %collective-permute-done.1.right_ref = bf16[2,641,128]{2,1,0:T(8,128)(2,1)} collective-permute-done((bf16[2,641,128]{2,1,0:T(8,128)(2,1)}, bf16[2,641,128]{2,1,0:T(8,128)(2,1)}, u32[]{:S(2)}, u32[]{:S(2)}) %collective-permute-start.1) | collective-permute-done | bytes 328224 | tf_op jit(solution)/shard_map/ppermute | solution.py:262
  19.7 5.0 %collective-permute-done.left_ref = bf16[2,641,128]{2,1,0:T(8,128)(2,1)} collective-permute-done((bf16[2,641,128]{2,1,0:T(8,128)(2,1)}, bf16[2,641,128]{2,1,0:T(8,128)(2,1)}, u32[]{:S(2)}, u32[]{:S(2)}) %collective-permute-start) | collective-permute-done | bytes 328224 | tf_op jit(solution)/shard_map/ppermute | solution.py:261
  24.7 32.4 %conv.1.normed_ref = bf16[24,641,128]{2,1,0:T(8,128)(2,1)} custom-call(bf16[24,641,128]{2,1,0:T(8,128)(2,1)} %bitcast.24, bf16[2,641,128]{2,1,0:T(8,128)(2,1)} %collective-permute-done.left_ref, bf16[2,641,128]{2,1,0:T(8,128)(2,1)} %collective-permute-done.1.right_ref, f32[656,25]{1,0:T(8,128)} %pad.4.taps_ref), custom_call_target="tpu_custom_call" | custom-call | tf_op jit(solution)/shard_map/conv/pallas_call | solution.py:264
  57.0 53.8 %main.1 = (bf16[24,641,128]{2,1,0:T(8,128)(2,1)}, f32[32,2,8,128]{3,2,1,0:T(8,128)}) custom-call(bf16[24,641,128]{2,1,0:T(8,128)(2,1)} %bitcast.25, bf16[24,641,128]{2,1,0:T(8,128)(2,1)} %conv.1.normed_ref, bf16[1282,641]{1,0:T(8,128)(2,1)} %bitcast.26, bf16[641,1282]{1,0:T(8,128)(2,1)} %bitcast.29, bf16[72,641]{1,0:T(8,128)(2,1)} %bitcast.31, ...), custom_call_target="tpu_custom_call" | custom-call | tf_op jit(solution)/shard_map/main/pallas_call | solution.py:281
  110.9 0.0 copy-start.4
  110.9 4.6 %copy.20 = bf16[1,641,24,128]{3,2,1,0:T(8,128)(2,1)} copy(bf16[1,641,24,128]{3,1,2,0:T(8,128)(2,1)} %bitcast.27) | data formatting | bytes 7876608
  115.5 0.0 copy-done.4
  115.5 0.7 slice_bitcast_fusion
  (2 shorter events, 0.0 us)
Async XLA Ops:
  0.6 11.7 %copy-start.5 = (f32[641,5,5]{0,2,1:T(8,128)S(1)}, f32[641,5,5]{0,2,1:T(8,128)}, u32[]{:S(2)}) copy-start(f32[641,5,5]{0,2,1:T(8,128)} %param.8) | copy-start | bytes 192304
  0.6 11.7 %copy-start.3 = (bf16[641,72]{0,1:T(8,128)(2,1)S(1)}, bf16[641,72]{0,1:T(8,128)(2,1)}, u32[]{:S(2)}) copy-start(bf16[641,72]{0,1:T(8,128)(2,1)} %param.11) | copy-start | bytes 276916
  0.7 12.7 %copy-start.2 = (f32[72,24,128]{2,1,0:T(8,128)S(1)}, f32[72,24,128]{2,1,0:T(8,128)}, u32[]{:S(2)}) copy-start(f32[72,24,128]{2,1,0:T(8,128)} %param.12) | copy-start | bytes 2654212
  3.4 2.0 %copy-start = (bf16[1,641,24,128]{3,1,2,0:T(8,128)(2,1)}, bf16[1,641,24,128]{3,1,2,0:T(8,128)(2,1)S(1)}, u32[]{:S(2)}) copy-start(bf16[1,641,24,128]{3,1,2,0:T(8,128)(2,1)S(1)} %copy.23) | copy-start | bytes 11814916
  3.4 11.1 %copy-start.1 = (bf16[641,1282]{1,0:T(8,128)(2,1)S(1)}, bf16[641,1282]{1,0:T(8,128)(2,1)}, u32[]{:S(2)}) copy-start(bf16[641,1282]{1,0:T(8,128)(2,1)} %param.9) | copy-start | bytes 4930576
  5.4 12.3 %copy-start.6 = (s32[24,128]{1,0:T(8,128)S(1)}, s32[24,128]{1,0:T(8,128)}, u32[]{:S(2)}) copy-start(s32[24,128]{1,0:T(8,128)} %param.13) | copy-start | bytes 36868
  6.3 13.4 %collective-permute-start.1 = (bf16[2,641,128]{2,1,0:T(8,128)(2,1)}, bf16[2,641,128]{2,1,0:T(8,128)(2,1)}, u32[]{:S(2)}, u32[]{:S(2)}) collective-permute-start(bf16[2,641,128]{2,1,0:T(8,128)(2,1)} %get-tuple-element.10), channel_id=1, source_target_pairs={{1,0},{2,1},{3,2},{4,3},{5,4},{6,5},{7,6},{0,7},{9,8},{10,9},{11,1... | collective-permute-start | bytes 984584 | tf_op jit(solution)/shard_map/ppermute | solution.py:262
  12.3 12.3 %collective-permute-start = (bf16[2,641,128]{2,1,0:T(8,128)(2,1)}, bf16[2,641,128]{2,1,0:T(8,128)(2,1)}, u32[]{:S(2)}, u32[]{:S(2)}) collective-permute-start(bf16[2,641,128]{2,1,0:T(8,128)(2,1)} %get-tuple-element.11), channel_id=1, source_target_pairs={{0,1},{1,2},{2,3},{3,4},{4,5},{5,6},{6,7},{7,0},{8,9},{9,10},{10,1... | collective-permute-start | bytes 984584 | tf_op jit(solution)/shard_map/ppermute | solution.py:261
  110.9 4.6 %copy-start.4 = (f32[32,2,8,128]{3,2,1,0:T(8,128)S(1)}, f32[32,2,8,128]{3,2,1,0:T(8,128)}, u32[]{:S(2)}) copy-start(f32[32,2,8,128]{3,2,1,0:T(8,128)} %get-tuple-element.5) | copy-start | bytes 786436

commit v3 on v2

--- a/solution.py
+++ b/solution.py
@@ -21,67 +21,100 @@
     return 0.5 * x * (1.0 + lax.erf(x * (0.5**0.5)))
 
 
-def conv_kernel(x_ref, left_ref, right_ref, taps_ref, normed_ref, conv_ref, sum_ref, wide_ref):
-    lon_len, channels, lat_len = x_ref.shape
-    half = left_ref.shape[0]
-    size = 2 * half + 1
+def conv_kernel(segments, *refs):
+    sources = refs[: len(segments)]
+    taps_ref, normed_ref, conv_ref, wide_ref = refs[len(segments) :]
+    channels, lat_len = sources[0].shape[1:]
+    rows_out = conv_ref.shape[0]
+    size = math.isqrt(taps_ref.shape[1])
+    half = size // 2
     full = channels // 16
     rest = channels - full * 16
-    lane = lax.broadcasted_iota(jnp.int32, (16, lat_len), 1)
-    sum_ref[...] = jnp.zeros_like(sum_ref)
-
-    def convolve(chan):
-        for q in range(size):
+    lane = lax.broadcasted_iota(jnp.int32, (8, lat_len), 1)
+    runs = []
+    at = 0
+    for group in sorted(set(segments)):
+        count = sum(r.shape[0] for r, g in zip(sources, segments) if g == group)
+        runs.append((at, count))
+        at += count
+
+    def fill(chan, kept):
+        at = 0
+        for ref in sources:
+            for i in range(ref.shape[0]):
+                wide_ref[at, 0:kept, :] = ref[i, chan, :].astype(jnp.float32)
+                at += 1
+
+    def convolve(first):
+        for part8 in range(2):
+            sub = slice(part8 * 8, part8 * 8 + 8)
+            chan = pl.ds(pl.multiple_of(first + part8 * 8, 8), 8)
             coef = [
-                jnp.broadcast_to(taps_ref[chan, p * size + q : p * size + q + 1], (16, lat_len))
-                for p in range(size)
+                jnp.broadcast_to(taps_ref[chan, t : t + 1], (8, lat_len))
+                for t in range(size * size)
             ]
-            shift = half - q
-            for i in range(lon_len):
-                part = coef[0] * wide_ref[i]
-                for p in range(1, size):
-                    part = part + coef[p] * wide_ref[i + p]
-                if shift != 0:
-                    part = pltpu.roll(part, shift % lat_len, 1)
-                    inside = lane >= shift if shift > 0 else lane < lat_len + shift
-                    part = jnp.where(inside, part, 0.0)
-                if q > 0:
-                    part = part + conv_ref[i, chan, :]
-                conv_ref[i, chan, :] = part
-                if q == size - 1:
-                    sum_ref[i] = sum_ref[i] + part[0:8] + part[8:16]
+            row = 0
+            for begin, count in runs:
+                for i in range(begin, begin + count - 2 * half):
+                    cells = [wide_ref[i + p, sub, :] for p in range(size)]
+                    total = None
+                    for q in range(size):
+                        part = coef[q] * cells[0]
+                        for p in range(1, size):
+                            part = part + coef[p * size + q] * cells[p]
+                        shift = half - q
+                        if shift != 0:
+                            part = pltpu.roll(part, shift % lat_len, 1)
+                            inside = lane >= shift if shift > 0 else lane < lat_len + shift
+                            part = jnp.where(inside, part, 0.0)
+                        total = part if total is None else total + part
+                    conv_ref[row, chan, :] = total
+                    row += 1
 
     def conv_block(block, carry):
-        chan = pl.ds(pl.multiple_of(block * 16, 16), 16)
-        for i in range(half):
-            wide_ref[i] = left_ref[i, chan, :].astype(jnp.float32)
-            wide_ref[half + lon_len + i] = right_ref[i, chan, :].astype(jnp.float32)
-        for i in range(lon_len):
-            wide_ref[half + i] = x_ref[i, chan, :].astype(jnp.float32)
-        convolve(chan)
+        first = pl.multiple_of(block * 16, 16)
+        fill(pl.ds(first, 16), 16)
+        convolve(first)
         return carry
 
     lax.fori_loop(0, full, conv_block, 0)
     if rest > 0:
         wide_ref[...] = jnp.zeros_like(wide_ref)
-        for i in range(half):
-            wide_ref[i, 0:rest, :] = left_ref[i, full * 16 : channels, :].astype(jnp.float32)
-            wide_ref[half + lon_len + i, 0:rest, :] = right_ref[i, full * 16 : channels, :].astype(
-                jnp.float32
-            )
-        for i in range(lon_len):
-            wide_ref[half + i, 0:rest, :] = x_ref[i, full * 16 : channels, :].astype(jnp.float32)
-        convolve(slice(full * 16, full * 16 + 16))
+        fill(slice(full * 16, channels), rest)
+        convolve(full * 16)
 
     def norm_row(row, carry):
-        center = jnp.sum(sum_ref[row], axis=0, keepdims=True) * (1.0 / channels)
-        shifted = conv_ref[row, 0:channels, :] - center
+        cells = conv_ref[row, 0:channels, :]
+        shifted = cells - jnp.sum(cells, axis=0, keepdims=True) * (1.0 / channels)
         square = jnp.sum(shifted * shifted, axis=0, keepdims=True)
         scale = lax.rsqrt(square * (1.0 / channels) + norm_eps)
         normed_ref[row] = (shifted * scale).astype(jnp.bfloat16)
         return carry
 
-    lax.fori_loop(0, lon_len, norm_row, 0)
+    lax.fori_loop(0, rows_out, norm_row, 0)
+
+
+def conv_norm(name, half, segments, sources, taps):
+    channels, lat_len = sources[0].shape[1:]
+    rows_in = sum(part.shape[0] for part in sources)
+    rows_out = rows_in - 2 * half * len(set(segments))
+    padded_c = taps.shape[0]
+    return pl.pallas_call(
+        functools.partial(conv_kernel, segments),
+        name=name,
+        out_shape=jax.ShapeDtypeStruct((rows_out, channels, lat_len), jnp.bfloat16),
+        in_specs=[VMEM_SPEC] * (len(sources) + 1),
+        out_specs=VMEM_SPEC,
+        scratch_shapes=[
+            pltpu.VMEM((rows_out, padded_c, lat_len), jnp.float32),
+            pltpu.VMEM((rows_in, 16, lat_len), jnp.float32),
+        ],
+        cost_estimate=pl.CostEstimate(
+            flops=2000 * rows_out * channels * lat_len,
+            bytes_accessed=4 * rows_in * channels * lat_len,
+            transcendentals=0,
+        ),
+    )(*sources, taps)
 
 
 def cuts_of(hid):
@@ -90,8 +123,8 @@
 
 
 def main_kernel(
-    groups, rows_at_once, scale, x_ref, normed_ref, w1_ref, w2_ref, dect_ref, dec_ref, observed_ref,
-    weight_ref, grad_ref, out_ref, block_ref, own_ref, others_ref, score_ref, term_ref, mine, got,
+    groups, rows_at_once, scale, x_ref, inner_ref, edge_ref, w1_ref, w2_ref, dect_ref, dec_ref, observed_ref,
+    weight_ref, grad_ref, out_ref, block_ref, own_ref, others_ref, score_ref, term_ref, tall_ref, mine, got,
     mine_sum, whole, pair_sems, sems,
 ):
     lon_len, channels, lat_len = x_ref.shape
@@ -117,8 +150,8 @@
     def joined(ref, step):
         return jnp.concatenate([ref[step * rows_at_once + r] for r in range(rows_at_once)], axis=1)
 
-    def mlp_step(step):
-        normed = joined(normed_ref, step)
+    def mlp_step(step, normed_ref, at):
+        normed = joined(normed_ref, at)
         out = joined(x_ref, step).astype(jnp.float32)
         for low, high in cuts_of(w1_ref.shape[0]):
             pre = jnp.dot(w1_ref[low:high, :], normed, preferred_element_type=jnp.float32)
@@ -141,19 +174,23 @@
             device_id=(lax.rem(member + j + 1, member_n), space), device_id_type=MESH,
         )
 
-    mlp_step(0)
+    mlp_step(0, edge_ref, 0)
     pl.semaphore_wait(barrier, n - 1)
     for j in range(member_n - 1):
         pair_copy(0, j).start()
 
     def mlp_loop(step, carry):
-        mlp_step(step)
+        mlp_step(step, inner_ref, step - 1)
         for j in range(member_n - 1):
             pair_copy(step, j).start()
         return carry
 
-    lax.fori_loop(1, steps, mlp_loop, 0)
+    lax.fori_loop(1, steps - 1, mlp_loop, 0)
+    mlp_step(steps - 1, edge_ref, 1)
+    for j in range(member_n - 1):
+        pair_copy(steps - 1, j).start()
     term_ref[...] = jnp.zeros_like(term_ref)
+    tall_ref[...] = jnp.zeros_like(tall_ref)
 
     def score_step(step, carry):
         for j in range(member_n - 1):
@@ -172,13 +209,14 @@
                 )
             weight = weight_ref[pl.ds(row, 1), :]
             score_ref[row] = (weight * (total - pair_sum / member_n)).astype(jnp.bfloat16)
-        term_ref[:, 0:channels] += lax.dot_general(
-            joined(score_ref, step), joined(block_ref, step), (((1,), (1,)), ((), ())),
+        tall_ref[...] += lax.dot_general(
+            joined(block_ref, step), joined(score_ref, step), (((1,), (1,)), ((), ())),
             preferred_element_type=jnp.float32,
         )
         return carry
 
     lax.fori_loop(0, steps, score_step, 0)
+    term_ref[:, 0:channels] = scale * jnp.transpose(tall_ref[...])
 
     def grad_step(step, carry):
         grad = jnp.dot(
@@ -188,17 +226,19 @@
             grad_ref[step * rows_at_once + r] = grad[:, r * lat_len : (r + 1) * lat_len]
         return carry
 
-    per = mine_sum.shape[0]
+    per = mine_sum.shape[0] // 8
     tall = term_ref.shape[0] // 8
     across = term_ref.shape[1] // 128
     for a in range(tall):
         for b in range(across):
             at = a * across + b
-            mine[at // per, at % per] = (
-                scale * term_ref[8 * a : 8 * a + 8, 128 * b : 128 * b + 128]
-            )
+            low = 8 * (at % per)
+            mine[at // per, low : low + 8, :] = term_ref[
+                8 * a : 8 * a + 8, 128 * b : 128 * b + 128
+            ].astype(jnp.bfloat16)
     for at in range(tall * across, n * per):
-        mine[at // per, at % per] = jnp.zeros((8, 128), jnp.float32)
+        low = 8 * (at % per)
+        mine[at // per, low : low + 8, :] = jnp.zeros((8, 128), jnp.bfloat16)
 
     def scatter_copy(e):
         other, device = peer(e)
@@ -231,9 +271,9 @@
     start(scatter_copy)
     lax.fori_loop(0, steps // 2, grad_step, 0)
     finish(scatter_copy)
-    total = mine[me]
+    total = mine[me].astype(jnp.float32)
     for e in range(n - 1):
-        total = total + got[e]
+        total = total + got[e].astype(jnp.float32)
     mine_sum[...] = total
     start(gather_copy)
     out_ref[me] = total
@@ -261,23 +301,15 @@
     left = lax.ppermute(x[lon_len - half :], "space", forth)
     right = lax.ppermute(x[:half], "space", back)
     taps = jnp.pad(depth_kernel.reshape(channels, size * size), ((0, padded_c - channels), (0, 0)))
-    normed = pl.pallas_call(
-        conv_kernel,
-        name="conv",
-        out_shape=jax.ShapeDtypeStruct((lon_len, channels, lat_len), jnp.bfloat16),
-        in_specs=[VMEM_SPEC] * 4,
-        out_specs=VMEM_SPEC,
-        scratch_shapes=[
-            pltpu.VMEM((lon_len, padded_c, lat_len), jnp.float32),
-            pltpu.VMEM((lon_len, 8, lat_len), jnp.float32),
-            pltpu.VMEM((lon_len + 2 * half, 16, lat_len), jnp.float32),
-        ],
-    )(x, left, right, taps)
+    inner = conv_norm("inner", half, (0,), (x,), taps)
+    edge = conv_norm(
+        "edge", half, (0, 0, 1, 1), (left, x[: 2 * half], x[lon_len - 2 * half :], right), taps
+    )
     weight = 4.0 + 8.0 * land_mask.astype(jnp.float32)
     wide_c = round_up(channels, 128)
     tiles = (outputs // 8) * (wide_c // 128)
     per = -(-tiles // n)
-    rows_at_once = 2
+    rows_at_once = half
     grad, summed = pl.pallas_call(
         functools.partial(
             main_kernel, (member_n, space_n), rows_at_once, 1.0 / math.sqrt(members * total_points)
@@ -285,9 +317,9 @@
         name="main",
         out_shape=(
             jax.ShapeDtypeStruct((lon_len, channels, lat_len), jnp.bfloat16),
-            jax.ShapeDtypeStruct((n, per, 8, 128), jnp.float32),
+            jax.ShapeDtypeStruct((n, per * 8, 128), jnp.float32),
         ),
-        in_specs=[VMEM_SPEC] * 8,
+        in_specs=[VMEM_SPEC] * 9,
         out_specs=[VMEM_SPEC] * 2,
         scratch_shapes=[
             pltpu.VMEM((lon_len, channels, lat_len), jnp.bfloat16),
@@ -295,16 +327,17 @@
             pltpu.VMEM((member_n - 1, lon_len, outputs, lat_len), jnp.bfloat16),
             pltpu.VMEM((lon_len, outputs, lat_len), jnp.bfloat16),
             pltpu.VMEM((outputs, wide_c), jnp.float32),
-            pltpu.VMEM((n, per, 8, 128), jnp.float32),
-            pltpu.VMEM((n - 1, per, 8, 128), jnp.float32),
-            pltpu.VMEM((per, 8, 128), jnp.float32),
-            pltpu.VMEM((n - 1, per, 8, 128), jnp.float32),
+            pltpu.VMEM((channels, outputs), jnp.float32),
+            pltpu.VMEM((n, per * 8, 128), jnp.bfloat16),
+            pltpu.VMEM((n - 1, per * 8, 128), jnp.bfloat16),
+            pltpu.VMEM((per * 8, 128), jnp.float32),
+            pltpu.VMEM((n - 1, per * 8, 128), jnp.float32),
             pltpu.SemaphoreType.DMA((2, member_n - 1, lon_len // rows_at_once)),
             pltpu.SemaphoreType.DMA((4, n - 1)),
         ],
         compiler_params=pltpu.CompilerParams(collective_id=0, has_side_effects=True),
     )(
-        x, normed, in_weight.T, out_weight.T, decoder_weight.T, decoder_weight,
+        x, inner, edge, in_weight.T, out_weight.T, decoder_weight.T, decoder_weight,
         jnp.transpose(observed, (1, 0, 2)), weight,
     )
     flat = summed.reshape(n * per, 8, 128)[:tiles].reshape(outputs // 8, wide_c // 128, 8, 128)

time: 116 us -> 114 us (0.983)
  waiting for transfers between devices: 6.42 us -> 0.01 us
  Pallas kernels: 86.2 us -> 90.6 us
    pallas_call x1 -> x2, Pallas kernels: 32.4 us -> 39.1 us  [conv_norm(): pl.pallas_call(functools.partial(conv_kernel, segments), name=name, out_s...]
    ppermute x1, waiting for transfers between devices: 4.97 us -> 0.01 us  [per_device(): left = lax.ppermute(x[lon_len - half:], 'space', forth)]
    pallas_call x1, Pallas kernels: 53.8 us -> 51.5 us  [per_device(): pl.pallas_call(functools.partial(main_kernel, (member_n, space_n), rows_a...]
    unnamed x19, local copies, waits for them, and re-layouts: 13.6 us -> 11.8 us
    ppermute x1, waiting for transfers between devices: 1.45 us -> 0.01 us  [per_device(): right = lax.ppermute(x[:half], 'space', back)]
    slice x0 -> x1, local copies, waits for them, and re-layouts: none -> 1.16 us  [per_device(): x[lon_len - 2 * half:]]
  transfers between devices with their start and end apart: 2 -> 2, of which waited for: 2 -> 0; matrix products, arithmetic and copies ran while one was open for 5% -> 6% of each run, Pallas kernels for 0% -> 23%
where the time goes in v3:
time: 114 us; the launch traced here: 113 us
  Pallas kernels  90.6 us (79%)
  local copies, waits for them, and re-layouts  15.5 us (14%)
  starting transfers between devices  6.04 us (5%)
    pallas_call x1, Pallas kernels, per_device(): pl.pallas_call(functools.partial(main_kernel, (member_n, space_n), rows_a...  51.5 us
    pallas_call x2, Pallas kernels, conv_norm(): pl.pallas_call(functools.partial(conv_kernel, segments), name=name, out_s...  39.1 us
    unnamed x19, local copies, waits for them, and re-layouts  11.8 us
    ppermute x1, starting transfers between devices, per_device(): right = lax.ppermute(x[:half], 'space', back)  6.03 us
  transfers between devices with their start and end apart: 2, of which 0 were waited for; matrix products, arithmetic and copies ran while one was open for 6% of the time, Pallas kernels for 23%

profile of v3, /device:TPU:0, one launch (start us, length us, event | category | flops | bytes accessed | tf_op | source)
XLA Modules:
  0.0 113.5 jit_solution(7281808142229252739)
XLA Ops:
  0.6 2.6 %copy.23 = bf16[1,641,24,128]{3,1,2,0:T(8,128)(2,1)S(1)} copy(bf16[1,641,24,128]{3,2,1,0:T(8,128)(2,1)} %param.7) | data formatting | bytes 7876608 | tf_op args[0]
  3.3 0.0 copy-start
  3.3 0.0 copy-start.6
  3.3 0.0 copy-start.5
  3.3 0.0 copy-start.3
  3.3 0.0 copy-start.2
  3.3 0.0 copy-start.1
  3.3 0.9 fusion
  4.2 6.0 %collective-permute-start.1 = (bf16[2,641,128]{2,1,0:T(8,128)(2,1)}, bf16[2,641,128]{2,1,0:T(8,128)(2,1)}, u32[]{:S(2)}, u32[]{:S(2)}) collective-permute-start(bf16[2,641,128]{2,1,0:T(8,128)(2,1)} %get-tuple-element.10), channel_id=1, source_target_pairs={{1,0},{2,1},{3,2},{4,3},{5,4},{6,5},{7,6},{0,7},{9,8},{10,9},{11,1... | collective-permute-start | bytes 984584 | tf_op jit(solution)/shard_map/ppermute | solution.py:302
  10.3 0.0 collective-permute-start
  10.3 0.0 copy-done
  10.3 1.2 %fusion.1 = (bf16[4,641,128]{2,1,0:T(8,128)(2,1)}, bf16[4,641,128]{2,1,0:T(8,128)(2,1)}) fusion(bf16[24,641,128]{2,1,0:T(8,128)(2,1)S(1)} %bitcast.24), kind=kLoop, calls=%fused_computation.5 | loop fusion | bytes 2625536 | tf_op jit(solution)/shard_map/slice | solution.py:306
  11.4 0.0 copy-done.6
  11.4 0.6 multiply_add_fusion.weight_ref
  12.0 0.0 copy-done.5
  12.1 0.0 copy-done.3
  12.1 0.8 copy.19.dec_ref
  12.9 0.2 copy.16
  13.0 0.0 copy-done.2
  13.1 1.1 copy.24
  14.2 0.0 copy-done.1
  14.2 2.6 %copy.17 = bf16[641,1282]{0,1:T(8,128)(2,1)} copy(bf16[641,1282]{1,0:T(8,128)(2,1)S(1)} %copy-done.1) | data formatting | bytes 3287048 | tf_op args[2]
  16.8 0.8 pad.4.refs_1_.refs_4_
  17.5 26.5 %inner.1.inner_ref = bf16[20,641,128]{2,1,0:T(8,128)(2,1)} custom-call(bf16[24,641,128]{2,1,0:T(8,128)(2,1)} %bitcast.25, f32[656,25]{1,0:T(8,128)} %pad.4.refs_1_.refs_4_), custom_call_target="tpu_custom_call" | custom-call | flops 3281920000 | bytes 7876608 | tf_op jit(solution)/shard_map/inner/pallas_call | solution.py:102
  44.0 0.0 collective-permute-done.1.refs_3_
  44.0 0.0 collective-permute-done.refs_0_
  44.0 12.6 %edge.1.edge_ref = bf16[4,641,128]{2,1,0:T(8,128)(2,1)} custom-call(bf16[2,641,128]{2,1,0:T(8,128)(2,1)} %collective-permute-done.refs_0_, bf16[4,641,128]{2,1,0:T(8,128)(2,1)} %get-tuple-element.13.refs_1_, bf16[4,641,128]{2,1,0:T(8,128)(2,1)} %get-tuple-element.12.refs_2_, bf16[2,641,128]{2,1,0:T(8,128)(2,1)} %collective-permute-done.1.refs_3_, ...), custom_call_target="tpu_custom_call" | custom-call | flops 656384000 | bytes 3938304 | tf_op jit(solution)/shard_map/edge/pallas_call | solution.py:102
  56.6 51.5 %main.1 = (bf16[24,641,128]{2,1,0:T(8,128)(2,1)}, f32[32,16,128]{2,1,0:T(8,128)}) custom-call(bf16[24,641,128]{2,1,0:T(8,128)(2,1)} %bitcast.26, bf16[20,641,128]{2,1,0:T(8,128)(2,1)} %inner.1.inner_ref, bf16[4,641,128]{2,1,0:T(8,128)(2,1)} %edge.1.edge_ref, bf16[1282,641]{1,0:T(8,128)(2,1)} %bitcast.27, bf16[641,1282]{1,0:T(8,128)(2,1)} %bitcast.30, ...), custom_call_target="tpu_custom_call" | custom-call | tf_op jit(solution)/shard_map/main/pallas_call | solution.py:313
  108.1 0.0 copy-start.4
  108.1 4.6 %copy.20 = bf16[1,641,24,128]{3,2,1,0:T(8,128)(2,1)} copy(bf16[1,641,24,128]{3,1,2,0:T(8,128)(2,1)} %bitcast.28) | data formatting | bytes 7876608
  112.7 0.0 copy-done.4
  112.8 0.7 slice_bitcast_fusion
  (2 shorter events, 0.0 us)
Async XLA Ops:
  3.3 7.0 %copy-start = (bf16[1,641,24,128]{3,1,2,0:T(8,128)(2,1)}, bf16[1,641,24,128]{3,1,2,0:T(8,128)(2,1)S(1)}, u32[]{:S(2)}) copy-start(bf16[1,641,24,128]{3,1,2,0:T(8,128)(2,1)S(1)} %copy.23) | copy-start | bytes 11814916
  3.3 8.2 %copy-start.6 = (s32[24,128]{1,0:T(8,128)S(1)}, s32[24,128]{1,0:T(8,128)}, u32[]{:S(2)}) copy-start(s32[24,128]{1,0:T(8,128)} %param.13) | copy-start | bytes 36868
  3.3 8.8 %copy-start.5 = (f32[641,5,5]{0,2,1:T(8,128)S(1)}, f32[641,5,5]{0,2,1:T(8,128)}, u32[]{:S(2)}) copy-start(f32[641,5,5]{0,2,1:T(8,128)} %param.8) | copy-start | bytes 192304
  3.3 8.8 %copy-start.3 = (bf16[641,72]{0,1:T(8,128)(2,1)S(1)}, bf16[641,72]{0,1:T(8,128)(2,1)}, u32[]{:S(2)}) copy-start(bf16[641,72]{0,1:T(8,128)(2,1)} %param.11) | copy-start | bytes 276916
  3.3 9.7 %copy-start.2 = (f32[72,24,128]{2,1,0:T(8,128)S(1)}, f32[72,24,128]{2,1,0:T(8,128)}, u32[]{:S(2)}) copy-start(f32[72,24,128]{2,1,0:T(8,128)} %param.12) | copy-start | bytes 2654212
  3.3 10.8 %copy-start.1 = (bf16[641,1282]{1,0:T(8,128)(2,1)S(1)}, bf16[641,1282]{1,0:T(8,128)(2,1)}, u32[]{:S(2)}) copy-start(bf16[641,1282]{1,0:T(8,128)(2,1)} %param.9) | copy-start | bytes 4930576
  4.2 39.8 %collective-permute-start.1 = (bf16[2,641,128]{2,1,0:T(8,128)(2,1)}, bf16[2,641,128]{2,1,0:T(8,128)(2,1)}, u32[]{:S(2)}, u32[]{:S(2)}) collective-permute-start(bf16[2,641,128]{2,1,0:T(8,128)(2,1)} %get-tuple-element.10), channel_id=1, source_target_pairs={{1,0},{2,1},{3,2},{4,3},{5,4},{6,5},{7,6},{0,7},{9,8},{10,9},{11,1... | collective-permute-start | bytes 984584 | tf_op jit(solution)/shard_map/ppermute | solution.py:302
  10.3 33.8 %collective-permute-start = (bf16[2,641,128]{2,1,0:T(8,128)(2,1)}, bf16[2,641,128]{2,1,0:T(8,128)(2,1)}, u32[]{:S(2)}, u32[]{:S(2)}) collective-permute-start(bf16[2,641,128]{2,1,0:T(8,128)(2,1)} %get-tuple-element.11), channel_id=1, source_target_pairs={{0,1},{1,2},{2,3},{3,4},{4,5},{5,6},{6,7},{7,0},{8,9},{9,10},{10,1... | collective-permute-start | bytes 984584 | tf_op jit(solution)/shard_map/ppermute | solution.py:301
  108.1 4.6 %copy-start.4 = (f32[32,16,128]{2,1,0:T(8,128)S(1)}, f32[32,16,128]{2,1,0:T(8,128)}, u32[]{:S(2)}) copy-start(f32[32,16,128]{2,1,0:T(8,128)} %get-tuple-element.5) | copy-start | bytes 786436

commit v4 on v3

--- a/solution.py
+++ b/solution.py
@@ -23,14 +23,30 @@
 
 def conv_kernel(segments, *refs):
     sources = refs[: len(segments)]
-    taps_ref, normed_ref, conv_ref, wide_ref = refs[len(segments) :]
+    taps_ref, normed_ref, conv_ref, wide_ref, spread_ref = refs[len(segments) :]
     channels, lat_len = sources[0].shape[1:]
     rows_out = conv_ref.shape[0]
-    size = math.isqrt(taps_ref.shape[1])
+    count_taps = taps_ref.shape[1] // 3
+    size = math.isqrt(count_taps)
     half = size // 2
     full = channels // 16
     rest = channels - full * 16
     lane = lax.broadcasted_iota(jnp.int32, (8, lat_len), 1)
+    taps = taps_ref[...]
+    high = taps.astype(jnp.bfloat16).astype(jnp.float32)
+    middle = (taps - high).astype(jnp.bfloat16).astype(jnp.float32)
+    low = taps - high - middle
+    column = lax.broadcasted_iota(jnp.int32, taps.shape, 1)
+    parts = jnp.where(
+        column < count_taps, high, jnp.where(column < 2 * count_taps, middle, low)
+    ).astype(jnp.bfloat16)
+    for t in range(count_taps):
+        at_row = lax.broadcasted_iota(jnp.int32, (3 * count_taps, lat_len), 0)
+        chosen = (at_row == t) | (at_row == t + count_taps) | (at_row == t + 2 * count_taps)
+        spread_ref[t] = jnp.dot(
+            parts, jnp.where(chosen, 1.0, 0.0).astype(jnp.bfloat16),
+            preferred_element_type=jnp.float32,
+        )
     runs = []
     at = 0
     for group in sorted(set(segments)):
@@ -49,10 +65,7 @@
         for part8 in range(2):
             sub = slice(part8 * 8, part8 * 8 + 8)
             chan = pl.ds(pl.multiple_of(first + part8 * 8, 8), 8)
-            coef = [
-                jnp.broadcast_to(taps_ref[chan, t : t + 1], (8, lat_len))
-                for t in range(size * size)
-            ]
+            coef = [spread_ref[t, chan, :] for t in range(size * size)]
             row = 0
             for begin, count in runs:
                 for i in range(begin, begin + count - 2 * half):
@@ -108,6 +121,7 @@
         scratch_shapes=[
             pltpu.VMEM((rows_out, padded_c, lat_len), jnp.float32),
             pltpu.VMEM((rows_in, 16, lat_len), jnp.float32),
+            pltpu.VMEM((taps.shape[1] // 3, padded_c, lat_len), jnp.float32),
         ],
         cost_estimate=pl.CostEstimate(
             flops=2000 * rows_out * channels * lat_len,
@@ -274,13 +288,13 @@
     total = mine[me].astype(jnp.float32)
     for e in range(n - 1):
         total = total + got[e].astype(jnp.float32)
-    mine_sum[...] = total
+    mine_sum[...] = total.astype(jnp.bfloat16)
     start(gather_copy)
-    out_ref[me] = total
+    out_ref[me] = mine_sum[...].astype(jnp.float32)
     lax.fori_loop(steps // 2, steps, grad_step, 0)
     finish(gather_copy)
     for e in range(n - 1):
-        out_ref[lax.rem(me + n - e - 1, n)] = whole[e]
+        out_ref[lax.rem(me + n - e - 1, n)] = whole[e].astype(jnp.float32)
 
 
 def per_device(features, depth_kernel, in_weight, out_weight, decoder_weight, observed, land_mask):
@@ -301,6 +315,7 @@
     left = lax.ppermute(x[lon_len - half :], "space", forth)
     right = lax.ppermute(x[:half], "space", back)
     taps = jnp.pad(depth_kernel.reshape(channels, size * size), ((0, padded_c - channels), (0, 0)))
+    taps = jnp.concatenate([taps, taps, taps], axis=1)
     inner = conv_norm("inner", half, (0,), (x,), taps)
     edge = conv_norm(
         "edge", half, (0, 0, 1, 1), (left, x[: 2 * half], x[lon_len - 2 * half :], right), taps
@@ -330,8 +345,8 @@
             pltpu.VMEM((channels, outputs), jnp.float32),
             pltpu.VMEM((n, per * 8, 128), jnp.bfloat16),
             pltpu.VMEM((n - 1, per * 8, 128), jnp.bfloat16),
-            pltpu.VMEM((per * 8, 128), jnp.float32),
-            pltpu.VMEM((n - 1, per * 8, 128), jnp.float32),
+            pltpu.VMEM((per * 8, 128), jnp.bfloat16),
+            pltpu.VMEM((n - 1, per * 8, 128), jnp.bfloat16),
             pltpu.SemaphoreType.DMA((2, member_n - 1, lon_len // rows_at_once)),
             pltpu.SemaphoreType.DMA((4, n - 1)),
         ],

time: 114 us -> 107 us (0.939)
  Pallas kernels: 90.6 us -> 83.7 us
    pallas_call x2, Pallas kernels: 39.1 us -> 34.3 us  [conv_norm(): pl.pallas_call(functools.partial(conv_kernel, segments), name=name, out_s...]
    pallas_call x1, Pallas kernels: 51.5 us -> 49.4 us  [per_device(): pl.pallas_call(functools.partial(main_kernel, (member_n, space_n), rows_a...]
  transfers between devices with their start and end apart: 2 -> 2, of which waited for: 0 -> 0; matrix products, arithmetic and copies ran while one was open for 6% -> 7% of each run, Pallas kernels for 23% -> 22%
where the time goes in v4:
time: 107 us
  Pallas kernels  83.7 us (78%)
  local copies, waits for them, and re-layouts  14.8 us (14%)
  starting transfers between devices  6.04 us (6%)
  other arithmetic  1.61 us (2%)
    pallas_call x1, Pallas kernels, per_device(): pl.pallas_call(functools.partial(main_kernel, (member_n, space_n), rows_a...  49.4 us
    pallas_call x2, Pallas kernels, conv_norm(): pl.pallas_call(functools.partial(conv_kernel, segments), name=name, out_s...  34.3 us
    unnamed x19, local copies, waits for them, and re-layouts  11.8 us
    ppermute x1, starting transfers between devices, per_device(): right = lax.ppermute(x[:half], 'space', back)  6.03 us
  transfers between devices with their start and end apart: 2, of which 0 were waited for; matrix products, arithmetic and copies ran while one was open for 7% of the time, Pallas kernels for 22%

profile of v4, /device:TPU:0, one launch (start us, length us, event | category | flops | bytes accessed | tf_op | source)
XLA Modules:
  0.0 106.8 jit_solution(3210869422496134948)
XLA Ops:
  0.6 2.6 %copy.23 = bf16[1,641,24,128]{3,1,2,0:T(8,128)(2,1)S(1)} copy(bf16[1,641,24,128]{3,2,1,0:T(8,128)(2,1)} %param.7) | data formatting | bytes 7876608 | tf_op args[0]
  3.3 0.0 copy-start
  3.3 0.0 copy-start.6
  3.3 0.0 copy-start.5
  3.3 0.0 copy-start.3
  3.3 0.0 copy-start.2
  3.3 0.0 copy-start.1
  3.3 0.9 fusion
  4.2 6.0 %collective-permute-start.1 = (bf16[2,641,128]{2,1,0:T(8,128)(2,1)}, bf16[2,641,128]{2,1,0:T(8,128)(2,1)}, u32[]{:S(2)}, u32[]{:S(2)}) collective-permute-start(bf16[2,641,128]{2,1,0:T(8,128)(2,1)} %get-tuple-element.10), channel_id=1, source_target_pairs={{1,0},{2,1},{3,2},{4,3},{5,4},{6,5},{7,6},{0,7},{9,8},{10,9},{11,1... | collective-permute-start | bytes 984584 | tf_op jit(solution)/shard_map/ppermute | solution.py:316
  10.3 0.0 collective-permute-start
  10.3 0.0 copy-done
  10.3 1.2 %fusion.1 = (bf16[4,641,128]{2,1,0:T(8,128)(2,1)}, bf16[4,641,128]{2,1,0:T(8,128)(2,1)}) fusion(bf16[24,641,128]{2,1,0:T(8,128)(2,1)S(1)} %bitcast.24), kind=kLoop, calls=%fused_computation.6 | loop fusion | bytes 2625536 | tf_op jit(solution)/shard_map/slice | solution.py:321
  11.4 0.0 copy-done.6
  11.4 0.6 multiply_add_fusion.weight_ref
  12.0 0.0 copy-done.5
  12.1 0.2 copy.16
  12.3 1.0 pad_maximum_fusion.refs_1_.refs_4_
  13.3 0.0 copy-done.3
  13.3 0.8 copy.19.dec_ref
  14.1 0.0 copy-done.2
  14.1 1.1 %copy.24 = f32[72,24,128]{2,0,1:T(8,128)} copy(f32[72,24,128]{2,1,0:T(8,128)S(1)} %copy-done.2) | data formatting | bytes 1769472 | tf_op args[5]
  15.2 0.0 copy-done.1
  15.2 2.6 %copy.17 = bf16[641,1282]{0,1:T(8,128)(2,1)} copy(bf16[641,1282]{1,0:T(8,128)(2,1)S(1)} %copy-done.1) | data formatting | bytes 3287048 | tf_op args[2]
  17.8 23.9 %inner.1.inner_ref = bf16[20,641,128]{2,1,0:T(8,128)(2,1)} custom-call(bf16[24,641,128]{2,1,0:T(8,128)(2,1)} %bitcast.25, f32[656,75]{1,0:T(8,128)} %pad_maximum_fusion.refs_1_.refs_4_), custom_call_target="tpu_custom_call" | custom-call | flops 3281920000 | bytes 7876608 | tf_op jit(solution)/shard_map/inner/pallas_call | solution.py:115
  41.7 0.0 collective-permute-done.1.refs_3_
  41.7 0.0 collective-permute-done.refs_0_
  41.7 10.4 %edge.1.edge_ref = bf16[4,641,128]{2,1,0:T(8,128)(2,1)} custom-call(bf16[2,641,128]{2,1,0:T(8,128)(2,1)} %collective-permute-done.refs_0_, bf16[4,641,128]{2,1,0:T(8,128)(2,1)} %get-tuple-element.13.refs_1_, bf16[4,641,128]{2,1,0:T(8,128)(2,1)} %get-tuple-element.12.refs_2_, bf16[2,641,128]{2,1,0:T(8,128)(2,1)} %collective-permute-done.1.refs_3_, ...), custom_call_target="tpu_custom_call" | custom-call | flops 656384000 | bytes 3938304 | tf_op jit(solution)/shard_map/edge/pallas_call | solution.py:115
  52.1 49.4 %main.1 = (bf16[24,641,128]{2,1,0:T(8,128)(2,1)}, f32[32,16,128]{2,1,0:T(8,128)}) custom-call(bf16[24,641,128]{2,1,0:T(8,128)(2,1)} %bitcast.26, bf16[20,641,128]{2,1,0:T(8,128)(2,1)} %inner.1.inner_ref, bf16[4,641,128]{2,1,0:T(8,128)(2,1)} %edge.1.edge_ref, bf16[1282,641]{1,0:T(8,128)(2,1)} %bitcast.27, bf16[641,1282]{1,0:T(8,128)(2,1)} %bitcast.30, ...), custom_call_target="tpu_custom_call" | custom-call | tf_op jit(solution)/shard_map/main/pallas_call | solution.py:328
  101.5 0.0 copy-start.4
  101.5 4.6 %copy.20 = bf16[1,641,24,128]{3,2,1,0:T(8,128)(2,1)} copy(bf16[1,641,24,128]{3,1,2,0:T(8,128)(2,1)} %bitcast.28) | data formatting | bytes 7876608
  106.1 0.0 copy-done.4
  106.1 0.7 slice_bitcast_fusion
  (3 shorter events, 0.1 us)
Async XLA Ops:
  3.3 7.0 %copy-start = (bf16[1,641,24,128]{3,1,2,0:T(8,128)(2,1)}, bf16[1,641,24,128]{3,1,2,0:T(8,128)(2,1)S(1)}, u32[]{:S(2)}) copy-start(bf16[1,641,24,128]{3,1,2,0:T(8,128)(2,1)S(1)} %copy.23) | copy-start | bytes 11814916
  3.3 8.2 %copy-start.6 = (s32[24,128]{1,0:T(8,128)S(1)}, s32[24,128]{1,0:T(8,128)}, u32[]{:S(2)}) copy-start(s32[24,128]{1,0:T(8,128)} %param.13) | copy-start | bytes 36868
  3.3 8.8 %copy-start.5 = (f32[641,5,5]{0,2,1:T(8,128)S(1)}, f32[641,5,5]{0,2,1:T(8,128)}, u32[]{:S(2)}) copy-start(f32[641,5,5]{0,2,1:T(8,128)} %param.8) | copy-start | bytes 192304
  3.3 10.0 %copy-start.3 = (bf16[641,72]{0,1:T(8,128)(2,1)S(1)}, bf16[641,72]{0,1:T(8,128)(2,1)}, u32[]{:S(2)}) copy-start(bf16[641,72]{0,1:T(8,128)(2,1)} %param.11) | copy-start | bytes 276916
  3.3 10.8 %copy-start.2 = (f32[72,24,128]{2,1,0:T(8,128)S(1)}, f32[72,24,128]{2,1,0:T(8,128)}, u32[]{:S(2)}) copy-start(f32[72,24,128]{2,1,0:T(8,128)} %param.12) | copy-start | bytes 2654212
  3.3 11.9 %copy-start.1 = (bf16[641,1282]{1,0:T(8,128)(2,1)S(1)}, bf16[641,1282]{1,0:T(8,128)(2,1)}, u32[]{:S(2)}) copy-start(bf16[641,1282]{1,0:T(8,128)(2,1)} %param.9) | copy-start | bytes 4930576
  4.2 37.5 %collective-permute-start.1 = (bf16[2,641,128]{2,1,0:T(8,128)(2,1)}, bf16[2,641,128]{2,1,0:T(8,128)(2,1)}, u32[]{:S(2)}, u32[]{:S(2)}) collective-permute-start(bf16[2,641,128]{2,1,0:T(8,128)(2,1)} %get-tuple-element.10), channel_id=1, source_target_pairs={{1,0},{2,1},{3,2},{4,3},{5,4},{6,5},{7,6},{0,7},{9,8},{10,9},{11,1... | collective-permute-start | bytes 984584 | tf_op jit(solution)/shard_map/ppermute | solution.py:316
  10.3 31.5 %collective-permute-start = (bf16[2,641,128]{2,1,0:T(8,128)(2,1)}, bf16[2,641,128]{2,1,0:T(8,128)(2,1)}, u32[]{:S(2)}, u32[]{:S(2)}) collective-permute-start(bf16[2,641,128]{2,1,0:T(8,128)(2,1)} %get-tuple-element.11), channel_id=1, source_target_pairs={{0,1},{1,2},{2,3},{3,4},{4,5},{5,6},{6,7},{7,0},{8,9},{9,10},{10,1... | collective-permute-start | bytes 984584 | tf_op jit(solution)/shard_map/ppermute | solution.py:315
  101.5 4.6 %copy-start.4 = (f32[32,16,128]{2,1,0:T(8,128)S(1)}, f32[32,16,128]{2,1,0:T(8,128)}, u32[]{:S(2)}) copy-start(f32[32,16,128]{2,1,0:T(8,128)} %get-tuple-element.5) | copy-start | bytes 786436

commit v5 on v4

--- a/solution.py
+++ b/solution.py
@@ -54,14 +54,16 @@
         runs.append((at, count))
         at += count
 
-    def fill(chan, kept):
-        at = 0
+    rows_in = wide_ref.shape[0] // 2
+
+    def fill(chan, kept, base):
+        at = base
         for ref in sources:
             for i in range(ref.shape[0]):
                 wide_ref[at, 0:kept, :] = ref[i, chan, :].astype(jnp.float32)
                 at += 1
 
-    def convolve(first):
+    def convolve(first, base):
         for part8 in range(2):
             sub = slice(part8 * 8, part8 * 8 + 8)
             chan = pl.ds(pl.multiple_of(first + part8 * 8, 8), 8)
@@ -69,7 +71,7 @@
             row = 0
             for begin, count in runs:
                 for i in range(begin, begin + count - 2 * half):
-                    cells = [wide_ref[i + p, sub, :] for p in range(size)]
+                    cells = [wide_ref[base + i + p, sub, :] for p in range(size)]
                     total = None
                     for q in range(size):
                         part = coef[q] * cells[0]
@@ -84,17 +86,22 @@
                     conv_ref[row, chan, :] = total
                     row += 1
 
-    def conv_block(block, carry):
-        first = pl.multiple_of(block * 16, 16)
-        fill(pl.ds(first, 16), 16)
-        convolve(first)
-        return carry
-
-    lax.fori_loop(0, full, conv_block, 0)
+    def conv_blocks(pair, carry):
+        firsts = [pl.multiple_of(pair * 32 + 16 * slot, 16) for slot in range(2)]
+        for slot in range(2):
+            fill(pl.ds(firsts[slot], 16), 16, slot * rows_in)
+        for slot in range(2):
+            convolve(firsts[slot], slot * rows_in)
+        return carry
+
+    lax.fori_loop(0, full // 2, conv_blocks, 0)
+    if full % 2:
+        fill(slice(full * 16 - 16, full * 16), 16, 0)
+        convolve(full * 16 - 16, 0)
     if rest > 0:
         wide_ref[...] = jnp.zeros_like(wide_ref)
-        fill(slice(full * 16, channels), rest)
-        convolve(full * 16)
+        fill(slice(full * 16, channels), rest, 0)
+        convolve(full * 16, 0)
 
     def norm_row(row, carry):
         cells = conv_ref[row, 0:channels, :]
@@ -120,7 +127,7 @@
         out_specs=VMEM_SPEC,
         scratch_shapes=[
             pltpu.VMEM((rows_out, padded_c, lat_len), jnp.float32),
-            pltpu.VMEM((rows_in, 16, lat_len), jnp.float32),
+            pltpu.VMEM((2 * rows_in, 16, lat_len), jnp.float32),
             pltpu.VMEM((taps.shape[1] // 3, padded_c, lat_len), jnp.float32),
         ],
         cost_estimate=pl.CostEstimate(

time: 107 us -> 105 us (0.981)
  Pallas kernels: 83.7 us -> 81.4 us
    pallas_call x2, Pallas kernels: 34.3 us -> 32.1 us  [conv_norm(): pl.pallas_call(functools.partial(conv_kernel, segments), name=name, out_s...]
where the time goes in v5:
time: 105 us
  Pallas kernels  81.4 us (78%)
  local copies, waits for them, and re-layouts  14.8 us (14%)
  starting transfers between devices  6.04 us (6%)
  other arithmetic  1.61 us (2%)
    pallas_call x1, Pallas kernels, per_device(): pl.pallas_call(functools.partial(main_kernel, (member_n, space_n), rows_a...  49.3 us
    pallas_call x2, Pallas kernels, conv_norm(): pl.pallas_call(functools.partial(conv_kernel, segments), name=name, out_s...  32.1 us
    unnamed x19, local copies, waits for them, and re-layouts  11.8 us
    ppermute x1, starting transfers between devices, per_device(): right = lax.ppermute(x[:half], 'space', back)  6.03 us
  transfers between devices with their start and end apart: 2, of which 0 were waited for; matrix products, arithmetic and copies ran while one was open for 7% of the time, Pallas kernels for 22%

profile of v5, /device:TPU:0, one launch (start us, length us, event | category | flops | bytes accessed | tf_op | source)
XLA Modules:
  0.0 104.5 jit_solution(16020817767647073084)
XLA Ops:
  0.6 2.6 %copy.23 = bf16[1,641,24,128]{3,1,2,0:T(8,128)(2,1)S(1)} copy(bf16[1,641,24,128]{3,2,1,0:T(8,128)(2,1)} %param.7) | data formatting | bytes 7876608 | tf_op args[0]
  3.3 0.0 copy-start
  3.3 0.0 copy-start.6
  3.3 0.0 copy-start.5
  3.3 0.0 copy-start.3
  3.3 0.0 copy-start.2
  3.3 0.0 copy-start.1
  3.3 0.9 fusion
  4.2 6.0 %collective-permute-start.1 = (bf16[2,641,128]{2,1,0:T(8,128)(2,1)}, bf16[2,641,128]{2,1,0:T(8,128)(2,1)}, u32[]{:S(2)}, u32[]{:S(2)}) collective-permute-start(bf16[2,641,128]{2,1,0:T(8,128)(2,1)} %get-tuple-element.10), channel_id=1, source_target_pairs={{1,0},{2,1},{3,2},{4,3},{5,4},{6,5},{7,6},{0,7},{9,8},{10,9},{11,1... | collective-permute-start | bytes 984584 | tf_op jit(solution)/shard_map/ppermute | solution.py:323
  10.3 0.0 collective-permute-start
  10.3 0.0 copy-done
  10.3 1.2 %fusion.1 = (bf16[4,641,128]{2,1,0:T(8,128)(2,1)}, bf16[4,641,128]{2,1,0:T(8,128)(2,1)}) fusion(bf16[24,641,128]{2,1,0:T(8,128)(2,1)S(1)} %bitcast.24), kind=kLoop, calls=%fused_computation.6 | loop fusion | bytes 2625536 | tf_op jit(solution)/shard_map/slice | solution.py:328
  11.4 0.0 copy-done.6
  11.4 0.6 multiply_add_fusion.weight_ref
  12.0 0.0 copy-done.5
  12.1 0.2 copy.16
  12.3 1.0 pad_maximum_fusion.refs_1_.refs_4_
  13.3 0.0 copy-done.3
  13.3 0.8 copy.19.dec_ref
  14.1 0.0 copy-done.2
  14.1 1.1 %copy.24 = f32[72,24,128]{2,0,1:T(8,128)} copy(f32[72,24,128]{2,1,0:T(8,128)S(1)} %copy-done.2) | data formatting | bytes 1769472 | tf_op args[5]
  15.2 0.0 copy-done.1
  15.2 2.6 %copy.17 = bf16[641,1282]{0,1:T(8,128)(2,1)} copy(bf16[641,1282]{1,0:T(8,128)(2,1)S(1)} %copy-done.1) | data formatting | bytes 3287048 | tf_op args[2]
  17.8 23.1 %inner.1.inner_ref = bf16[20,641,128]{2,1,0:T(8,128)(2,1)} custom-call(bf16[24,641,128]{2,1,0:T(8,128)(2,1)} %bitcast.25, f32[656,75]{1,0:T(8,128)} %pad_maximum_fusion.refs_1_.refs_4_), custom_call_target="tpu_custom_call" | custom-call | flops 3281920000 | bytes 7876608 | tf_op jit(solution)/shard_map/inner/pallas_call | solution.py:122
  40.9 0.0 collective-permute-done.1.refs_3_
  40.9 0.0 collective-permute-done.refs_0_
  40.9 9.0 %edge.1.edge_ref = bf16[4,641,128]{2,1,0:T(8,128)(2,1)} custom-call(bf16[2,641,128]{2,1,0:T(8,128)(2,1)} %collective-permute-done.refs_0_, bf16[4,641,128]{2,1,0:T(8,128)(2,1)} %get-tuple-element.13.refs_1_, bf16[4,641,128]{2,1,0:T(8,128)(2,1)} %get-tuple-element.12.refs_2_, bf16[2,641,128]{2,1,0:T(8,128)(2,1)} %collective-permute-done.1.refs_3_, ...), custom_call_target="tpu_custom_call" | custom-call | flops 656384000 | bytes 3938304 | tf_op jit(solution)/shard_map/edge/pallas_call | solution.py:122
  49.9 49.3 %main.1 = (bf16[24,641,128]{2,1,0:T(8,128)(2,1)}, f32[32,16,128]{2,1,0:T(8,128)}) custom-call(bf16[24,641,128]{2,1,0:T(8,128)(2,1)} %bitcast.26, bf16[20,641,128]{2,1,0:T(8,128)(2,1)} %inner.1.inner_ref, bf16[4,641,128]{2,1,0:T(8,128)(2,1)} %edge.1.edge_ref, bf16[1282,641]{1,0:T(8,128)(2,1)} %bitcast.27, bf16[641,1282]{1,0:T(8,128)(2,1)} %bitcast.30, ...), custom_call_target="tpu_custom_call" | custom-call | tf_op jit(solution)/shard_map/main/pallas_call | solution.py:335
  99.2 0.0 copy-start.4
  99.2 4.6 %copy.20 = bf16[1,641,24,128]{3,2,1,0:T(8,128)(2,1)} copy(bf16[1,641,24,128]{3,1,2,0:T(8,128)(2,1)} %bitcast.28) | data formatting | bytes 7876608
  103.8 0.0 copy-done.4
  103.8 0.7 slice_bitcast_fusion
  (3 shorter events, 0.1 us)
Async XLA Ops:
  3.3 7.0 %copy-start = (bf16[1,641,24,128]{3,1,2,0:T(8,128)(2,1)}, bf16[1,641,24,128]{3,1,2,0:T(8,128)(2,1)S(1)}, u32[]{:S(2)}) copy-start(bf16[1,641,24,128]{3,1,2,0:T(8,128)(2,1)S(1)} %copy.23) | copy-start | bytes 11814916
  3.3 8.2 %copy-start.6 = (s32[24,128]{1,0:T(8,128)S(1)}, s32[24,128]{1,0:T(8,128)}, u32[]{:S(2)}) copy-start(s32[24,128]{1,0:T(8,128)} %param.13) | copy-start | bytes 36868
  3.3 8.8 %copy-start.5 = (f32[641,5,5]{0,2,1:T(8,128)S(1)}, f32[641,5,5]{0,2,1:T(8,128)}, u32[]{:S(2)}) copy-start(f32[641,5,5]{0,2,1:T(8,128)} %param.8) | copy-start | bytes 192304
  3.3 10.0 %copy-start.3 = (bf16[641,72]{0,1:T(8,128)(2,1)S(1)}, bf16[641,72]{0,1:T(8,128)(2,1)}, u32[]{:S(2)}) copy-start(bf16[641,72]{0,1:T(8,128)(2,1)} %param.11) | copy-start | bytes 276916
  3.3 10.8 %copy-start.2 = (f32[72,24,128]{2,1,0:T(8,128)S(1)}, f32[72,24,128]{2,1,0:T(8,128)}, u32[]{:S(2)}) copy-start(f32[72,24,128]{2,1,0:T(8,128)} %param.12) | copy-start | bytes 2654212
  3.3 11.9 %copy-start.1 = (bf16[641,1282]{1,0:T(8,128)(2,1)S(1)}, bf16[641,1282]{1,0:T(8,128)(2,1)}, u32[]{:S(2)}) copy-start(bf16[641,1282]{1,0:T(8,128)(2,1)} %param.9) | copy-start | bytes 4930576
  4.2 36.7 %collective-permute-start.1 = (bf16[2,641,128]{2,1,0:T(8,128)(2,1)}, bf16[2,641,128]{2,1,0:T(8,128)(2,1)}, u32[]{:S(2)}, u32[]{:S(2)}) collective-permute-start(bf16[2,641,128]{2,1,0:T(8,128)(2,1)} %get-tuple-element.10), channel_id=1, source_target_pairs={{1,0},{2,1},{3,2},{4,3},{5,4},{6,5},{7,6},{0,7},{9,8},{10,9},{11,1... | collective-permute-start | bytes 984584 | tf_op jit(solution)/shard_map/ppermute | solution.py:323
  10.3 30.6 %collective-permute-start = (bf16[2,641,128]{2,1,0:T(8,128)(2,1)}, bf16[2,641,128]{2,1,0:T(8,128)(2,1)}, u32[]{:S(2)}, u32[]{:S(2)}) collective-permute-start(bf16[2,641,128]{2,1,0:T(8,128)(2,1)} %get-tuple-element.11), channel_id=1, source_target_pairs={{0,1},{1,2},{2,3},{3,4},{4,5},{5,6},{6,7},{7,0},{8,9},{9,10},{10,1... | collective-permute-start | bytes 984584 | tf_op jit(solution)/shard_map/ppermute | solution.py:322
  99.2 4.6 %copy-start.4 = (f32[32,16,128]{2,1,0:T(8,128)S(1)}, f32[32,16,128]{2,1,0:T(8,128)}, u32[]{:S(2)}) copy-start(f32[32,16,128]{2,1,0:T(8,128)} %get-tuple-element.5) | copy-start | bytes 786436
